TPU v7x, 32 devices: a whole 2x2x4 slice. The times are simulated.
32 devices in a mesh: groups: 2 (over x), lat: 16 (over z, y, core).
Axes of the slice: x: 2, y: 2, z: 4, core: 2. Of those that a mesh axis runs over, the one named last changes fastest.
Arguments:
- harmonic_right_sides: float32 [16, 8, 2, 640, 640], P('groups', None, None, 'lat'), parts along dimension 0, may hold values from -0.625 to 0.625
- azimuthal_number_list: int32 [640], replicated, may hold values from 0 to 639, each once
- parallel_arrangement: int32 [160], replicated, may hold values from 0 to 159, each once
- polar_basis_values: bfloat16 [640, 160, 640], P('lat'), may hold values from -0.25 to 0.25
- eigen_forward_matrix: float32 [8, 8], replicated, may hold values from -2 to 2
- eigen_back_matrix: float32 [8, 8], replicated, may hold values from -2 to 2
- eigen_wave_celerity: float32 [8], replicated, may hold values from 1e-06 to 0.001
- thermal_response_matrix: float32 [8, 8], replicated, may hold values from -2 to 2
Outputs:
- grid_out: bfloat16 [16, 8, 160, 2560], P('groups', None, 'lat'), parts along dimension 0
There are 2 independent parts, one for each index of `groups`. A program takes and returns all parts, laid end to end along the dimension named above; an argument that names none is the same for every part. Nothing has to cross between parts.
Inputs may be any that keep to these rules, and one draw needn't show every extreme that they name: `azimuthal_number_list`: every wavenumber 0 to 639 is held by exactly one slot. `parallel_arrangement`: every latitude 0 to 159 appears at exactly one grid row.
All inputs are finite; a program needn't handle non-finite values.
Results may differ from a plain program's by a relative error of at most 0.0062.
Values may be sent and summed in bfloat16 or wider, within the bound.
No kernel may reach another device: no remote copies, remote signals or barrier semaphores. Data moves between devices by JAX's collectives and lax.ppermute only.
A program may use at most 64 MiB of HBM per device.

v0:
```python
import jax
import jax.numpy as jnp
from jax import lax
from jax.sharding import PartitionSpec as P

NLON = 2560


full_circle_radians = 6.283185307179586


def wave_table(azimuthal_number_list, nlon):
    longitude = jnp.arange(nlon, dtype=jnp.int32)
    coupled_product = azimuthal_number_list[:, None] * longitude[None, :] % nlon
    phase_angle = coupled_product.astype(jnp.float32) * (full_circle_radians / nlon)
    weight = jnp.where(azimuthal_number_list == 0, 1.0, 2.0).astype(jnp.float32)[:, None]
    return jnp.stack([weight * jnp.cos(phase_angle), -weight * jnp.sin(phase_angle)], 0).astype(
        jnp.bfloat16
    )


def implicit_update_quantities(
    harmonic_right_sides,
    position_labels,
    eigen_forward_matrix,
    eigen_back_matrix,
    eigen_wave_celerity,
    thermal_response_matrix,
):
    offsets = jnp.arange(harmonic_right_sides.shape[-1], dtype=jnp.int32)
    total_n = position_labels[:, None] + offsets[None, :]
    inside = total_n < harmonic_right_sides.shape[-1]
    degree = total_n.astype(jnp.float32)
    laplace_eigen = degree * (degree + 1.0)
    maximal_order = lax.Precision.HIGHEST
    modal_part = jnp.einsum(
        "ml,lcsk->mcsk", eigen_forward_matrix, harmonic_right_sides[0], precision=maximal_order
    )
    damped = modal_part / (1.0 + eigen_wave_celerity[:, None, None, None] * laplace_eigen)
    spreading_rate_plane = jnp.einsum(
        "kp,phli->khli", eigen_back_matrix, damped, precision=maximal_order
    )
    thermal_quantity = harmonic_right_sides[1] - jnp.einsum(
        "kp,phli->khli", thermal_response_matrix, spreading_rate_plane, precision=maximal_order
    )
    quantity_pile = jnp.concatenate(
        [spreading_rate_plane[None], thermal_quantity[None], harmonic_right_sides[2:]], 0
    )
    return jnp.where(inside, quantity_pile, jnp.zeros_like(quantity_pile)).astype(jnp.bfloat16)


def per_device(
    harmonic_right_sides,
    azimuthal_number_list,
    parallel_arrangement,
    polar_basis_values,
    eigen_forward_matrix,
    eigen_back_matrix,
    eigen_wave_celerity,
    thermal_response_matrix,
):
    field_count = harmonic_right_sides.shape[0]
    vertical_level_count = harmonic_right_sides.shape[1]
    slot_count = polar_basis_values.shape[0]
    nlat = polar_basis_values.shape[1]
    waves = polar_basis_values.shape[2]
    device_count = lax.axis_size("lat")
    lat_dev = nlat // device_count
    my_index = lax.axis_index("lat")
    position_labels = lax.dynamic_slice_in_dim(
        azimuthal_number_list, my_index * slot_count, slot_count
    )
    harmonic_weights = implicit_update_quantities(
        harmonic_right_sides,
        position_labels,
        eigen_forward_matrix,
        eigen_back_matrix,
        eigen_wave_celerity,
        thermal_response_matrix,
    )
    row_count = field_count * vertical_level_count
    flat = harmonic_weights.reshape(row_count * 2, slot_count, waves)
    natural = jnp.einsum(
        "rsk,slk->rsl", flat, polar_basis_values, preferred_element_type=jnp.float32
    )
    fourier = jnp.take(natural, parallel_arrangement, axis=2).astype(jnp.bfloat16)
    fourier = fourier.reshape(row_count, 2, slot_count, nlat)
    table = wave_table(azimuthal_number_list, NLON)
    grid_out = jnp.einsum(
        "icsr,csj->irj",
        lax.all_to_all(fourier, "lat", split_axis=3, concat_axis=2, tiled=True),
        table,
        preferred_element_type=jnp.float32,
    ).astype(jnp.bfloat16)
    return grid_out.reshape(field_count, vertical_level_count, lat_dev, grid_out.shape[-1])


def solution(mesh):
    in_specs = (
        P("groups", None, None, "lat", None),
        P(),
        P(),
        P("lat", None, None),
        P(),
        P(),
        P(),
        P(),
    )
    out_specs = P("groups", None, "lat", None)
    return jax.shard_map(
        per_device, mesh=mesh, in_specs=in_specs, out_specs=out_specs, check_vma=False
    )
```

profile of v0, /device:TPU:13, one launch (start us, length us, event | category | flops | bytes accessed | tf_op | source)
XLA Modules:
  0.0 100.4 jit_solution(11709728243222653447)
XLA Ops:
  0.0 2.1 %fusion.34 = (f32[1,8,2,40,640]{4,3,2,1,0:T(8,128)S(1)}, f32[1,8,2,40,640]{4,3,2,1,0:T(8,128)S(1)}) fusion(f32[8,8,2,40,640]{4,3,2,1,0:T(8,128)} %param.8), kind=kLoop, calls=%fused_computation.48 | loop fusion | bytes 6553600 | tf_op jit(solution)/shard_map/slice | solution.py:37
  2.2 6.5 %slice.11 = bf16[6,8,2,40,640]{4,3,2,1,0:T(8,128)(2,1)} slice(f32[8,8,2,40,640]{4,3,2,1,0:T(8,128)} %param.8), slice={[2:8], [0:8], [0:2], [0:40], [0:640]} | slice | bytes 9830400 | tf_op jit(solution)/shard_map/slice | solution.py:47
  9.0 0.1 multiply_add_fusion
  9.2 1.8 %fusion.19 = f32[8,2,40,640]{3,0,2,1:T(8,128)S(1)} fusion(f32[1,8,2,40,640]{4,3,2,1,0:T(8,128)S(1)} %get-tuple-element.5, f32[8,8]{1,0:T(8,128)S(1)} %copy-done), kind=kOutput, calls=%fused_computation.28 | convolution fusion | flops 39321600 | bytes 3277056 | tf_op jit(solution)/shard_map/ml,lcsk->mcsk/dot_general | solution.py:36
  11.1 1.6 %fusion.22 = f32[2,40,640,8]{2,3,1,0:T(8,128)S(1)} fusion(f32[8,2,40,640]{3,0,2,1:T(8,128)S(1)} %fusion.19, f32[8,40,640]{2,0,1:T(8,128)S(1)} %multiply_add_fusion, f32[8,8]{1,0:T(8,128)S(1)} %copy-done.8), kind=kOutput, calls=%fused_computation.31 | convolution fusion | flops 39731200 | bytes 4096256 | tf_op jit(solution)/shard_map/kp,phli->khli/dot_general | solution.py:40
  12.7 2.1 %fusion.18 = bf16[1,8,2,40,640]{4,1,3,2,0:T(8,128)(2,1)S(1)} fusion(f32[1,8,2,40,640]{4,3,2,1,0:T(8,128)S(1)} %get-tuple-element.6, f32[2,40,640,8]{2,3,1,0:T(8,128)S(1)} %fusion.22, f32[8,8]{1,0:T(8,128)S(1)} %copy-done.5), kind=kOutput, calls=%fused_computation.26 | convolution fusion | flops 40140800 | bytes 4096256 | tf_op jit(solution)/shard_map/kp,phli->khli/dot_general | solution.py:43
  14.8 0.3 copy.49
  15.1 0.7 pad_maximum_fusion
  15.8 5.9 %fusion.14 = bf16[128,40,160]{0,2,1:T(8,128)(2,1)S(1)} fusion(bf16[40,160,640]{2,1,0:T(8,128)(2,1)} %param.11, bf16[128,40,640]{2,1,0:T(8,128)(2,1)S(1)} %bitcast.69, pred[40,640]{1,0:T(8,128)(4,1)S(1)} %fusion.27), kind=kOutput, calls=%fused_computation.23 | convolution fusion | flops 1051852800 | bytes 16409600 | tf_op jit(solution)/shard_map/rsk,slk->rsl/dot_general | solution.py:83
  21.7 0.6 copy.52
  22.4 1.0 gather_fusion
  23.3 5.9 %copy.53 = bf16[128,40,160]{2,1,0:T(8,128)(2,1)} copy(bf16[128,40,160]{0,1,2:T(8,128)(2,1)S(1)} %bitcast.67) | data formatting | bytes 3276800 | tf_op jit(solution)/shard_map/jit(_take)/gather | solution.py:86
  29.2 3.7 %select_convert_fusion = bf16[64,2,40,160]{3,2,1,0:T(8,128)(2,1)} fusion(bf16[64,2,40,160]{3,2,1,0:T(8,128)(2,1)} %bitcast.68, pred[160]{0:T(512)(128)(4,1)S(1)} %compare_and_fusion), kind=kLoop, calls=%fused_computation.21 | loop fusion | flops 819200 | bytes 3276960 | tf_op jit(solution)/shard_map/convert_element_type | solution.py:86
  33.0 6.5 %copy.54 = bf16[64,2,40,160]{0,2,1,3:T(8,128)(2,1)S(1)} copy(bf16[64,2,40,160]{3,2,1,0:T(8,128)(2,1)} %select_convert_fusion) | data formatting | bytes 3276800 | tf_op jit(solution)/shard_map/convert_element_type | solution.py:86
  39.5 3.1 %reshape.177 = bf16[16,2,25600]{2,1,0:T(2,128)(2,1)} reshape(bf16[160,2,40,64]{3,2,1,0:T(8,128)(2,1)S(1)} %bitcast.66) | data formatting | bytes 3276800
  42.6 6.5 %all-to-all-start = ((bf16[16,2,25600]{2,1,0:T(2,128)(2,1)}), bf16[16,2,25600]{2,1,0:T(2,128)(2,1)}, u32[]{:S(2)}, u32[]{:S(2)}) async-start(bf16[16,2,25600]{2,1,0:T(2,128)(2,1)} %reshape.177), calls=%async_computation | async-start | bytes 3276800 | tf_op jit(solution)/shard_map/all_to_all | solution.py:91
  49.1 29.7 %multiply_convert_fusion.1 = (bf16[1,640,2560]{2,1,0:T(8,128)(2,1)}, bf16[1,640,2560]{2,1,0:T(8,128)(2,1)}) fusion(s32[640]{0:T(1024)S(1)} %copy-done.4, f32[640]{0:T(1024)S(1)} %get-tuple-element.9, f32[640]{0:T(1024)S(1)} %get-tuple-element.10), kind=kLoop, calls=%fused_computation.14 | loop fusion | flops 21299200 | bytes 6561280 | tf_op jit(solution)/shard_map/convert
  78.8 8.0 %all-to-all-done = bf16[16,2,25600]{2,1,0:T(2,128)(2,1)} async-done(((bf16[16,2,25600]{2,1,0:T(2,128)(2,1)}), bf16[16,2,25600]{2,1,0:T(2,128)(2,1)}, u32[]{:S(2)}, u32[]{:S(2)}) %all-to-all-start) | async-done | bytes 1638432 | tf_op jit(solution)/shard_map/all_to_all | solution.py:91
  86.8 3.7 %reshape.178 = bf16[160,2,40,64]{3,2,1,0:T(8,128)(2,1)S(1)} reshape(bf16[16,2,25600]{2,1,0:T(2,128)(2,1)} %all-to-all-done) | data formatting | bytes 3276800
  90.6 0.9 copy.56
  91.5 1.0 %copy-done.2 = bf16[1,640,2560]{2,1,0:T(8,128)(2,1)S(1)} copy-done((bf16[1,640,2560]{2,1,0:T(8,128)(2,1)S(1)}, bf16[1,640,2560]{2,1,0:T(8,128)(2,1)}, u32[]{:S(2)}) %copy-start.2) | copy-done | bytes 3276824
  92.5 1.0 copy-done.3
  93.5 4.9 %fusion.13 = bf16[8,8,10,2560]{3,1,0,2:T(8,128)(2,1)S(1)} fusion(bf16[64,2,640,10]{0,2,3,1:T(8,128)(2,1)S(1)} %bitcast.71, bf16[1,640,2560]{2,1,0:T(8,128)(2,1)S(1)} %copy-done.3, bf16[1,640,2560]{2,1,0:T(8,128)(2,1)S(1)} %copy-done.2), kind=kOutput, calls=%fused_computation.22 | convolution fusion | flops 4199219200 | bytes 11468800 | tf_op jit(solution)/shard_map/icsr,csj->irj/dot_general | solution.py:89
  98.4 2.0 %copy.58 = bf16[8,8,10,2560]{3,1,2,0:T(8,128)(2,1)} copy(bf16[8,8,10,2560]{3,1,0,2:T(8,128)(2,1)S(1)} %fusion.13) | data formatting | bytes 6553600 | tf_op jit(solution)/shard_map/reshape | solution.py:95
  (29 shorter events, 0.4 us)
Async XLA Ops:
  0.0 9.2 %copy-start = (f32[8,8]{1,0:T(8,128)S(1)}, f32[8,8]{1,0:T(8,128)}, u32[]{:S(2)}) copy-start(f32[8,8]{1,0:T(8,128)} %param.12) | copy-start | bytes 772
  2.2 6.6 %copy-start.4 = (s32[640]{0:T(1024)S(1)}, s32[640]{0:T(1024)}, u32[]{:S(2)}) copy-start(s32[640]{0:T(1024)} %param.9) | copy-start | bytes 7684
  2.2 6.8 %copy-start.6 = (s32[160]{0:T(256)S(1)}, s32[160]{0:T(256)}, u32[]{:S(2)}) copy-start(s32[160]{0:T(256)} %param.10) | copy-start | bytes 1924
  2.2 6.8 %copy-start.7 = (f32[8]{0:T(128)S(1)}, f32[8]{0:T(128)}, u32[]{:S(2)}) copy-start(f32[8]{0:T(128)} %param.14) | copy-start | bytes 100
  8.7 2.3 %copy-start.8 = (f32[8,8]{1,0:T(8,128)S(1)}, f32[8,8]{1,0:T(8,128)}, u32[]{:S(2)}) copy-start(f32[8,8]{1,0:T(8,128)} %param.13) | copy-start | bytes 772
  11.0 1.6 %copy-start.5 = (f32[8,8]{1,0:T(8,128)S(1)}, f32[8,8]{1,0:T(8,128)}, u32[]{:S(2)}) copy-start(f32[8,8]{1,0:T(8,128)} %param.15) | copy-start | bytes 772
  11.0 4.0 %slice-start = ((s8[4915200]{0:T(1024)(128)(4,1)}), s8[4194304]{0:T(1024)(128)(4,1)S(1)}, s32[]{:S(2)}) async-start(s8[4915200]{0:T(1024)(128)(4,1)} %bitcast.63), calls=%async_computation.1 | async-start | bytes 8388608
  12.6 2.5 %slice-start.1 = ((s8[4915200]{0:T(1024)(128)(4,1)}), s8[720896]{0:T(1024)(128)(4,1)S(1)}, s32[]{:S(2)}) async-start(s8[4915200]{0:T(1024)(128)(4,1)} %bitcast.63), calls=%async_computation.2 | async-start | bytes 1441792
  42.6 44.2 %all-to-all-start = ((bf16[16,2,25600]{2,1,0:T(2,128)(2,1)}), bf16[16,2,25600]{2,1,0:T(2,128)(2,1)}, u32[]{:S(2)}, u32[]{:S(2)}) async-start(bf16[16,2,25600]{2,1,0:T(2,128)(2,1)} %reshape.177), calls=%async_computation | async-start | bytes 3276800 | tf_op jit(solution)/shard_map/all_to_all | solution.py:91
  90.6 1.9 %copy-start.2 = (bf16[1,640,2560]{2,1,0:T(8,128)(2,1)S(1)}, bf16[1,640,2560]{2,1,0:T(8,128)(2,1)}, u32[]{:S(2)}) copy-start(bf16[1,640,2560]{2,1,0:T(8,128)(2,1)} %get-tuple-element.7) | copy-start | bytes 9830404
  90.6 2.9 %copy-start.3 = (bf16[1,640,2560]{2,1,0:T(8,128)(2,1)S(1)}, bf16[1,640,2560]{2,1,0:T(8,128)(2,1)}, u32[]{:S(2)}) copy-start(bf16[1,640,2560]{2,1,0:T(8,128)(2,1)} %get-tuple-element.8) | copy-start | bytes 9830404
  93.5 6.9 %copy-start.1 = (f32[8,8]{1,0:T(8,128)S(1)}, f32[8,8]{1,0:T(8,128)}, u32[]{:S(2)}) copy-start(f32[8,8]{1,0:T(8,128)} %param.12) | copy-start | bytes 772
where the time goes:
time: 101 us; the launch traced here: 100 us
  local copies, waits for them, and re-layouts  34.9 us (35%)
  other arithmetic  34.5 us (34%)
  matrix products  16.3 us (16%)
  waiting for transfers between devices  7.97 us (8%)
  starting transfers between devices  6.52 us (6%)
    another operation x1, other arithmetic  29.7 us
    unnamed x24, local copies, waits for them, and re-layouts  8.91 us
    all_to_all x1, waiting for transfers between devices, per_device(): lax.all_to_all(fourier, 'lat', split_axis=3, concat_axis=2, tiled=True)  7.97 us
    gather x2, local copies, waits for them, and re-layouts, per_device(): jnp.take(natural, parallel_arrangement, axis=2).astype(jnp.bfloat16)  6.89 us
    slice x1, local copies, waits for them, and re-layouts, implicit_update_quantities(): harmonic_right_sides[2:]  6.54 us
    all_to_all x1, starting transfers between devices, per_device(): lax.all_to_all(fourier, 'lat', split_axis=3, concat_axis=2, tiled=True)  6.52 us
    convert_element_type x1, local copies, waits for them, and re-layouts, per_device(): jnp.take(natural, parallel_arrangement, axis=2).astype(jnp.bfloat16)  6.52 us
    dot_general x1, matrix products, per_device(): jnp.einsum('rsk,slk->rsl', flat, polar_basis_values, preferred_element_ty...  5.88 us
  transfers between devices with their start and end apart: 1, of which 1 were waited for; matrix products, arithmetic and copies ran while one was open for 30% of the time, Pallas kernels for 0%

commit v1 on v0

v1 whole, which is shorter than its diff:
```python
import functools
import jax
import jax.numpy as jnp
from jax import lax
from jax.experimental import pallas as pl
from jax.experimental.pallas import tpu as pltpu
from jax.sharding import PartitionSpec as P

NLON = 2560
LANES = 128
SUBLANES = 8
full_circle_radians = 6.283185307179586


def wave_table(azimuthal_number_list, nlon):
    longitude = jnp.arange(nlon, dtype=jnp.int32)
    coupled_product = azimuthal_number_list[:, None] * longitude[None, :] % nlon
    phase_angle = coupled_product.astype(jnp.float32) * (full_circle_radians / nlon)
    weight = jnp.where(azimuthal_number_list == 0, 1.0, 2.0).astype(jnp.float32)[:, None]
    return jnp.stack([weight * jnp.cos(phase_angle), -weight * jnp.sin(phase_angle)], 0).astype(
        jnp.bfloat16
    )


def implicit_update_quantities(rhs, position_labels, forward, back, celerity, thermal):
    offsets = jnp.arange(rhs.shape[-1], dtype=jnp.int32)
    total_n = position_labels[:, None] + offsets[None, :]
    inside = total_n < rhs.shape[-1]
    degree = total_n.astype(jnp.float32)
    laplace_eigen = degree * (degree + 1.0)
    high = lax.Precision.HIGHEST
    modal_part = jnp.einsum("ml,lcsk->mcsk", forward, rhs[0], precision=high)
    damped = modal_part / (1.0 + celerity[:, None, None, None] * laplace_eigen)
    divergence = jnp.einsum("kp,phli->khli", back, damped, precision=high)
    temperature = rhs[1] - jnp.einsum("kp,phli->khli", thermal, divergence, precision=high)
    pile = jnp.concatenate([divergence[None], temperature[None], rhs[2:]], 0)
    return jnp.where(inside, pile, jnp.zeros_like(pile)).astype(jnp.bfloat16)


def per_device_plain(rhs, azimuthal, arrangement, polar, forward, back, celerity, thermal):
    fields, levels = rhs.shape[:2]
    slots, nlat, waves = polar.shape
    lat_dev = nlat // lax.axis_size("lat")
    labels = lax.dynamic_slice_in_dim(azimuthal, lax.axis_index("lat") * slots, slots)
    coeffs = implicit_update_quantities(rhs, labels, forward, back, celerity, thermal)
    rows = fields * levels
    natural = jnp.einsum(
        "rsk,slk->rsl",
        coeffs.reshape(rows * 2, slots, waves),
        polar,
        preferred_element_type=jnp.float32,
    )
    fourier = jnp.take(natural, arrangement, axis=2).astype(jnp.bfloat16)
    fourier = fourier.reshape(rows, 2, slots, nlat)
    grid_out = jnp.einsum(
        "icsr,csj->irj",
        lax.all_to_all(fourier, "lat", split_axis=3, concat_axis=2, tiled=True),
        wave_table(azimuthal, NLON),
        preferred_element_type=jnp.float32,
    ).astype(jnp.bfloat16)
    return grid_out.reshape(fields, levels, lat_dev, NLON)


def legendre_kernel(
    azim_ref, arr_ref, fwd_ref, back_ref, cel_ref, therm_ref, *refs, levels, slots, nlat, waves
):
    tiles = waves // LANES
    rhs_refs = refs[:tiles]
    polar_ref, out_ref, nat_ref, upd_ref = refs[tiles:]
    rows = rhs_refs[0].shape[0]
    step = pl.program_id(0)
    first = lax.axis_index("lat") * slots + step * SUBLANES

    sub = lax.broadcasted_iota(jnp.int32, (SUBLANES, LANES), 0)
    lane = lax.broadcasted_iota(jnp.int32, (SUBLANES, LANES), 1)
    label = jnp.zeros((SUBLANES, LANES), jnp.int32)
    for s in range(SUBLANES):
        label = jnp.where(sub == s, azim_ref[first + s], label)

    for t in range(tiles):
        degree = (label + lane + t * LANES).astype(jnp.float32)
        laplace = degree * (degree + 1.0)
        den = [1.0 / (1.0 + cel_ref[m] * laplace) for m in range(levels)]
        ref = rhs_refs[t]
        x0 = [[ref[l * 2 + c] for c in range(2)] for l in range(levels)]
        damped = []
        for m in range(levels):
            acc = [fwd_ref[m, 0] * x0[0][c] for c in range(2)]
            for l in range(1, levels):
                acc = [acc[c] + fwd_ref[m, l] * x0[l][c] for c in range(2)]
            damped.append([acc[c] * den[m] for c in range(2)])
        div = []
        for l in range(levels):
            acc = [back_ref[l, 0] * damped[0][c] for c in range(2)]
            for m in range(1, levels):
                acc = [acc[c] + back_ref[l, m] * damped[m][c] for c in range(2)]
            div.append(acc)
            for c in range(2):
                upd_ref[t, pl.ds((l * 2 + c) * SUBLANES, SUBLANES), :] = acc[c]
        for l in range(levels):
            acc = [therm_ref[l, 0] * div[0][c] for c in range(2)]
            for q in range(1, levels):
                acc = [acc[c] + therm_ref[l, q] * div[q][c] for c in range(2)]
            for c in range(2):
                upd_ref[t, pl.ds(((levels + l) * 2 + c) * SUBLANES, SUBLANES), :] = (
                    ref[(levels + l) * 2 + c] - acc[c]
                )

    solved = 4 * levels
    rest = rows - solved
    for s in range(SUBLANES):
        room = waves - azim_ref[first + s]
        pieces = []
        for t in range(tiles):
            flat = rhs_refs[t].reshape(rows * SUBLANES, LANES)
            parts = []
            for c in range(2):
                parts.append(
                    upd_ref[t, pl.ds(c * SUBLANES + s, solved // 2, stride=2 * SUBLANES), :]
                )
                parts.append(
                    flat[pl.ds((solved + c) * SUBLANES + s, rest // 2, stride=2 * SUBLANES), :]
                )
            piece = jnp.concatenate(parts, 0)
            k = lax.broadcasted_iota(jnp.int32, piece.shape, 1) + t * LANES
            pieces.append(jnp.where(k < room, piece, 0.0).astype(jnp.bfloat16))
        coeffs = jnp.concatenate(pieces, 1)
        product = lax.dot_general(
            polar_ref[s], coeffs, (((1,), (1,)), ((), ())), preferred_element_type=jnp.float32
        )
        nat_ref[pl.ds((step * SUBLANES + s) * nlat, nlat), :] = product

    @pl.when(step == pl.num_programs(0) - 1)
    def _():
        half = LANES // 2
        low = lax.broadcasted_iota(jnp.int32, (slots, LANES), 1) < half

        def pair(p, carry):
            a = nat_ref[pl.ds(arr_ref[2 * p], slots, stride=nlat), :]
            b = nat_ref[pl.ds(arr_ref[2 * p + 1], slots, stride=nlat), :]
            real = jnp.where(low, a, pltpu.roll(b, half, 1))
            imag = jnp.where(low, pltpu.roll(a, half, 1), b)
            out_ref[p] = jnp.concatenate([real, imag], 0).astype(jnp.bfloat16)
            return carry

        lax.fori_loop(0, nlat // 2, pair, 0, unroll=4)


def legendre(rhs, azimuthal, arrangement, polar, forward, back, celerity, thermal):
    fields, levels = rhs.shape[:2]
    slots, nlat, waves = polar.shape
    rows = fields * levels * 2
    tiles = waves // LANES
    smem = pl.BlockSpec(memory_space=pltpu.SMEM)
    flat = rhs.reshape(rows, slots, waves)
    rhs_specs = [
        pl.BlockSpec((rows, SUBLANES, LANES), functools.partial(lambda t, i: (0, i, t), t))
        for t in range(tiles)
    ]
    return pl.pallas_call(
        functools.partial(
            legendre_kernel, levels=levels, slots=slots, nlat=nlat, waves=waves
        ),
        grid=(slots // SUBLANES,),
        in_specs=[smem] * 6
        + rhs_specs
        + [pl.BlockSpec((SUBLANES, nlat, waves), lambda i: (i, 0, 0))],
        out_specs=pl.BlockSpec((nlat // 2, 2 * slots, LANES), lambda i: (0, 0, 0)),
        out_shape=jax.ShapeDtypeStruct((nlat // 2, 2 * slots, LANES), jnp.bfloat16),
        scratch_shapes=[
            pltpu.VMEM((slots * nlat, LANES), jnp.float32),
            pltpu.VMEM((tiles, 4 * levels * SUBLANES, LANES), jnp.float32),
        ],
        compiler_params=pltpu.CompilerParams(vmem_limit_bytes=36 * 1024 * 1024),
        name="legendre",
    )(azimuthal, arrangement, forward, back, celerity, thermal, *([flat] * tiles), polar)


def table_kernel(azim_ref, out_ref, *, slots, nlon):
    blocks = nlon // LANES
    m = azim_ref[0]
    lane = lax.broadcasted_iota(jnp.int32, (slots, LANES), 1)
    unit = full_circle_radians / nlon
    fine = ((m * lane) % nlon).astype(jnp.float32) * unit
    coarse = ((m * lane) % blocks).astype(jnp.float32) * (unit * LANES)
    weight = jnp.where(m == 0, 1.0, 2.0)
    cos_fine = weight * jnp.cos(fine)
    sin_fine = weight * jnp.sin(fine)
    cos_coarse = jnp.cos(coarse)
    sin_coarse = jnp.sin(coarse)
    for b in range(blocks):
        cc = cos_coarse[:, b : b + 1]
        sc = sin_coarse[:, b : b + 1]
        real = cos_fine * cc - sin_fine * sc
        imag = -(sin_fine * cc + cos_fine * sc)
        out_ref[0, :, b * LANES : (b + 1) * LANES] = jnp.concatenate([real, imag], 0).astype(
            jnp.bfloat16
        )


def table(azimuthal, devices, slots):
    spread = jnp.broadcast_to(azimuthal.reshape(devices, slots, 1), (devices, slots, LANES))
    return pl.pallas_call(
        functools.partial(table_kernel, slots=slots, nlon=NLON),
        grid=(devices,),
        in_specs=[pl.BlockSpec((1, slots, LANES), lambda d: (d, 0, 0))],
        out_specs=pl.BlockSpec((1, 2 * slots, NLON), lambda d: (d, 0, 0)),
        out_shape=jax.ShapeDtypeStruct((devices, 2 * slots, NLON), jnp.bfloat16),
        compiler_params=pltpu.CompilerParams(vmem_limit_bytes=16 * 1024 * 1024),
        name="table",
    )(spread)


def grid_kernel(x_ref, tab_ref, out_ref, lhs_ref, acc_ref, *, lat_dev):
    depth = tab_ref.shape[0]
    tiles = tab_ref.shape[1] // LANES
    half = LANES // 2

    @pl.when(pl.program_id(0) == 0)
    def _():
        for p in range(lat_dev // 2):
            block = x_ref[:, p].reshape(depth, LANES)
            lhs_ref[pl.ds(p * LANES, LANES), :] = block.T

    product = jnp.dot(lhs_ref[...], tab_ref[...], preferred_element_type=jnp.float32)
    for t in range(tiles):
        acc_ref[t] = product[:, t * LANES : (t + 1) * LANES]

    for t in range(tiles):
        for i in range(half):
            out_ref[i, :, t * LANES : (t + 1) * LANES] = acc_ref[
                t, pl.ds(i, lat_dev, stride=half), :
            ].astype(jnp.bfloat16)


def grid_product(received, tab, lat_dev, block=512):
    devices = received.shape[0]
    depth = tab.shape[0] * tab.shape[1]
    half = LANES // 2
    x = received.reshape(devices, lat_dev // 2, depth // devices, LANES)
    return pl.pallas_call(
        functools.partial(grid_kernel, lat_dev=lat_dev),
        grid=(NLON // block,),
        in_specs=[
            pl.BlockSpec(x.shape, lambda j: (0, 0, 0, 0)),
            pl.BlockSpec((depth, block), lambda j: (0, j)),
        ],
        out_specs=pl.BlockSpec((half, lat_dev, block), lambda j: (0, 0, j)),
        out_shape=jax.ShapeDtypeStruct((half, lat_dev, NLON), jnp.bfloat16),
        scratch_shapes=[
            pltpu.VMEM((lat_dev * half, depth), jnp.bfloat16),
            pltpu.VMEM((block // LANES, lat_dev * half, LANES), jnp.float32),
        ],
        compiler_params=pltpu.CompilerParams(vmem_limit_bytes=24 * 1024 * 1024),
        name="grid_product",
    )(x, tab.reshape(depth, NLON))


def per_device(rhs, azimuthal, arrangement, polar, forward, back, celerity, thermal):
    fields, levels = rhs.shape[:2]
    slots, nlat, waves = polar.shape
    devices = lax.axis_size("lat")
    lat_dev = nlat // devices
    packed = legendre(rhs, azimuthal, arrangement, polar, forward, back, celerity, thermal)
    packed = packed.reshape(devices, lat_dev * slots, LANES)
    received = lax.all_to_all(packed, "lat", split_axis=0, concat_axis=0, tiled=True)
    tab = table(azimuthal, devices, slots)
    grid_out = grid_product(received, tab, lat_dev)
    return grid_out.reshape(fields, levels, lat_dev, NLON)


def solution(mesh):
    in_specs = (
        P("groups", None, None, "lat", None),
        P(),
        P(),
        P("lat", None, None),
        P(),
        P(),
        P(),
        P(),
    )
    out_specs = P("groups", None, "lat", None)

    def body(rhs, azimuthal, arrangement, polar, *matrices):
        slots, nlat, waves = polar.shape
        lat_dev = nlat // lax.axis_size("lat")
        fits = (
            slots % SUBLANES == 0
            and waves % LANES == 0
            and lat_dev % 2 == 0
            and 2 * rhs.shape[0] * rhs.shape[1] == LANES
            and rhs.shape[0] > 2
        )
        form = per_device if fits else per_device_plain
        return form(rhs, azimuthal, arrangement, polar, *matrices)

    return jax.shard_map(
        body, mesh=mesh, in_specs=in_specs, out_specs=out_specs, check_vma=False
    )
```

time: 101 us -> 87 us (0.86)
  Pallas kernels: 0 us -> 35.4 us
  other arithmetic: 34.5 us -> 0 us
  waiting for transfers between devices: 7.97 us -> 27.9 us
  local copies, waits for them, and re-layouts: 34.9 us -> 16.8 us
  matrix products: 16.3 us -> 0 us
    pallas_call x0 -> x3, Pallas kernels: none -> 35.4 us  [the longest x1 17.1 us: legendre(): pl.pallas_call(functools.partial(legendre_kernel, levels=levels, slots=sl...]
    another operation x1 -> x0, other arithmetic: 29.7 us -> none
    all_to_all x1, waiting for transfers between devices: 7.97 us -> 27.9 us  [per_device(): lax.all_to_all(packed, 'lat', split_axis=0, concat_axis=0, tiled=True)]
    dot_general x5 -> x0, matrix products: 16.3 us -> none  [the longest x1 5.88 us: per_device(): jnp.einsum('rsk,slk->rsl', flat, polar_basis_values, preferred_element_ty...]
    slice x2 -> x0, local copies, waits for them, and re-layouts: 8.68 us -> none  [the longest x1 6.54 us: implicit_update_quantities(): harmonic_right_sides[2:]]
    gather x2 -> x0, local copies, waits for them, and re-layouts: 6.89 us -> none  [per_device(): jnp.take(natural, parallel_arrangement, axis=2).astype(jnp.bfloat16)]
    convert_element_type x1 -> x0, local copies, waits for them, and re-layouts: 6.52 us -> none  [per_device(): jnp.take(natural, parallel_arrangement, axis=2).astype(jnp.bfloat16)]
    unnamed x24 -> x20, local copies, waits for them, and re-layouts: 8.91 us -> 13 us
  transfers between devices with their start and end apart: 1 -> 1, of which waited for: 1 -> 1; matrix products, arithmetic and copies ran while one was open for 30% -> 0% of each run, Pallas kernels for 0% -> 8%
where the time goes in v1:
time: 87 us; the launch traced here: 86.6 us
  Pallas kernels  35.4 us (41%)
  waiting for transfers between devices  27.9 us (32%)
  local copies, waits for them, and re-layouts  16.8 us (19%)
  starting transfers between devices  6.52 us (7%)
    all_to_all x1, waiting for transfers between devices, per_device(): lax.all_to_all(packed, 'lat', split_axis=0, concat_axis=0, tiled=True)  27.9 us
    pallas_call x1, Pallas kernels, legendre(): pl.pallas_call(functools.partial(legendre_kernel, levels=levels, slots=sl...  17.1 us
    unnamed x20, local copies, waits for them, and re-layouts  13 us
    pallas_call x1, Pallas kernels, grid_product(): pl.pallas_call(functools.partial(grid_kernel, lat_dev=lat_dev), grid=(NLO...  11.5 us
    pallas_call x1, Pallas kernels, table(): pl.pallas_call(functools.partial(table_kernel, slots=slots, nlon=NLON), g...  6.72 us
    all_to_all x1, starting transfers between devices, per_device(): lax.all_to_all(packed, 'lat', split_axis=0, concat_axis=0, tiled=True)  6.52 us
    reshape x1, local copies, waits for them, and re-layouts, per_device(): return grid_out.reshape(fields, levels, lat_dev, NLON)  3.57 us
  transfers between devices with their start and end apart: 1, of which 1 were waited for; matrix products, arithmetic and copies ran while one was open for 0% of the time, Pallas kernels for 8%

profile of v1, /device:TPU:13, one launch (start us, length us, event | category | flops | bytes accessed | tf_op | source)
XLA Modules:
  0.0 86.6 jit_solution(10876979082792134608)
XLA Ops:
  0.0 0.0 copy-start.2
  0.0 3.3 %copy-done.2 = bf16[40,160,640]{2,1,0:T(8,128)(2,1)S(1)} copy-done((bf16[40,160,640]{2,1,0:T(8,128)(2,1)S(1)}, bf16[40,160,640]{2,1,0:T(8,128)(2,1)}, u32[]{:S(2)}) %copy-start.2) | copy-done | bytes 8192024
  3.3 0.0 copy-start.3
  3.3 0.7 copy-done.3
  4.0 0.0 copy-start.5
  4.0 0.7 copy-done.5
  4.7 0.0 copy-start.6
  4.7 0.7 copy-done.6
  5.4 0.0 copy-start.7
  5.4 0.7 copy-done.7
  6.1 0.7 copy-done.8
  6.8 0.7 copy-done.9
  7.4 17.1 %legendre.1 = bf16[80,80,128]{2,1,0:T(8,128)(2,1)} custom-call(s32[640]{0:T(1024)S(1)} %copy-done.3, s32[160]{0:T(256)S(1)} %copy-done.8, f32[8,8]{1,0:T(8,128)S(1)} %copy-done.5, f32[8,8]{1,0:T(8,128)S(1)} %copy-done.6, f32[8]{0:T(128)S(1)} %copy-done.9, f32[8,8]{1,0:T(8,128)S(1)} %copy-done.7, f32[128,40,640]{2,1,0:T(8,128)} %bitcast.8, ...), custom_call_target="tpu_custom_call" | custom-call | tf_op jit(solution)/shard_map/legendre/pallas_call | solution.py:160
  24.5 6.5 %all-to-all-start = ((bf16[16,400,128]{2,1,0:T(8,128)(2,1)}), bf16[16,400,128]{2,1,0:T(8,128)(2,1)S(1)}, u32[]{:S(2)}, u32[]{:S(2)}) async-start(bf16[16,400,128]{2,1,0:T(8,128)(2,1)} %bitcast.1), calls=%async_computation | async-start | bytes 3276800 | tf_op jit(solution)/shard_map/all_to_all | solution.py:266
  31.1 0.0 copy-done.4
  31.1 0.1 broadcast_in_dim.7
  31.2 0.1 broadcast_in_dim.8.azim_ref
  31.3 6.7 %table.1 = bf16[16,80,2560]{2,1,0:T(8,128)(2,1)S(1)} custom-call(s32[16,40,128]{2,1,0:T(8,128)S(1)} %broadcast_in_dim.8.azim_ref), custom_call_target="tpu_custom_call" | custom-call | tf_op jit(solution)/shard_map/table/pallas_call | solution.py:203
  38.0 0.0 copy-start
  38.0 2.7 %copy-done = bf16[16,80,2560]{2,1,0:T(8,128)(2,1)} copy-done((bf16[16,80,2560]{2,1,0:T(8,128)(2,1)}, bf16[16,80,2560]{2,1,0:T(8,128)(2,1)S(1)}, u32[]{:S(2)}) %copy-start) | copy-done | bytes 6553624
  40.8 27.9 %all-to-all-done = bf16[16,400,128]{2,1,0:T(8,128)(2,1)S(1)} async-done(((bf16[16,400,128]{2,1,0:T(8,128)(2,1)}), bf16[16,400,128]{2,1,0:T(8,128)(2,1)S(1)}, u32[]{:S(2)}, u32[]{:S(2)}) %all-to-all-start) | async-done | bytes 1638432 | tf_op jit(solution)/shard_map/all_to_all | solution.py:266
  68.7 2.9 %copy-done.1 = bf16[16,80,2560]{2,1,0:T(8,128)(2,1)S(1)} copy-done((bf16[16,80,2560]{2,1,0:T(8,128)(2,1)S(1)}, bf16[16,80,2560]{2,1,0:T(8,128)(2,1)}, u32[]{:S(2)}) %copy-start.1) | copy-done | bytes 6553624
  71.5 11.5 %grid_product.1 = bf16[64,10,2560]{2,1,0:T(8,128)(2,1)S(1)} custom-call(bf16[16,5,80,128]{3,2,1,0:T(8,128)(2,1)S(1)} %bitcast.7, bf16[1280,2560]{1,0:T(8,128)(2,1)S(1)} %bitcast.5), custom_call_target="tpu_custom_call" | custom-call | tf_op jit(solution)/shard_map/grid_product/pallas_call | solution.py:241
  83.0 3.6 %copy.9 = bf16[8,8,10,2560]{3,1,2,0:T(8,128)(2,1)} copy(bf16[8,8,10,2560]{3,2,1,0:T(8,128)(2,1)S(1)} %bitcast.6) | data formatting | bytes 6553600 | tf_op jit(solution)/shard_map/reshape | solution.py:269
  (4 shorter events, 0.0 us)
Async XLA Ops:
  0.0 3.3 %copy-start.2 = (bf16[40,160,640]{2,1,0:T(8,128)(2,1)S(1)}, bf16[40,160,640]{2,1,0:T(8,128)(2,1)}, u32[]{:S(2)}) copy-start(bf16[40,160,640]{2,1,0:T(8,128)(2,1)} %refs_5_.1) | copy-start | bytes 24576004
  3.3 0.7 copy-start.3
  4.0 0.7 copy-start.5
  4.7 0.7 copy-start.6
  5.4 0.7 copy-start.7
  6.1 0.7 copy-start.8
  6.8 0.7 copy-start.9
  7.4 23.7 %copy-start.4 = (s32[640]{0:T(1024)S(1)}, s32[640]{0:T(1024)}, u32[]{:S(2)}) copy-start(s32[640]{0:T(1024)} %azim_ref.1) | copy-start | bytes 7684
  24.5 44.1 %all-to-all-start = ((bf16[16,400,128]{2,1,0:T(8,128)(2,1)}), bf16[16,400,128]{2,1,0:T(8,128)(2,1)S(1)}, u32[]{:S(2)}, u32[]{:S(2)}) async-start(bf16[16,400,128]{2,1,0:T(8,128)(2,1)} %bitcast.1), calls=%async_computation | async-start | bytes 3276800 | tf_op jit(solution)/shard_map/all_to_all | solution.py:266
  38.0 2.7 %copy-start = (bf16[16,80,2560]{2,1,0:T(8,128)(2,1)}, bf16[16,80,2560]{2,1,0:T(8,128)(2,1)S(1)}, u32[]{:S(2)}) copy-start(bf16[16,80,2560]{2,1,0:T(8,128)(2,1)S(1)} %table.1) | copy-start | bytes 19660804
  68.7 2.9 %copy-start.1 = (bf16[16,80,2560]{2,1,0:T(8,128)(2,1)S(1)}, bf16[16,80,2560]{2,1,0:T(8,128)(2,1)}, u32[]{:S(2)}) copy-start(bf16[16,80,2560]{2,1,0:T(8,128)(2,1)} %copy-done) | copy-start | bytes 19660804

commit v2 on v1

--- a/solution.py
+++ b/solution.py
@@ -62,73 +62,88 @@
 
 
 def legendre_kernel(
-    azim_ref, arr_ref, fwd_ref, back_ref, cel_ref, therm_ref, *refs, levels, slots, nlat, waves
+    azim_hbm, arr_hbm, fwd_hbm, back_hbm, cel_hbm, therm_hbm, *refs, levels, slots, nlat, waves
 ):
     tiles = waves // LANES
     rhs_refs = refs[:tiles]
-    polar_ref, out_ref, nat_ref, upd_ref = refs[tiles:]
+    polar_ref, out_ref, nat_ref, pad_ref = refs[tiles : tiles + 4]
+    scalars, sems = refs[tiles + 4 : -1], refs[-1]
+    azim_ref, arr_ref, fwd_ref, back_ref, cel_ref, therm_ref = scalars
+    sources = (azim_hbm, arr_hbm, fwd_hbm, back_hbm, cel_hbm, therm_hbm)
+    copies = [
+        pltpu.make_async_copy(src, dst, sems.at[i])
+        for i, (src, dst) in enumerate(zip(sources, scalars))
+    ]
     rows = rhs_refs[0].shape[0]
+    pitch = row_pitch()
+    apart = slot_pitch(nlat)
     step = pl.program_id(0)
+
+    @pl.when(step == 0)
+    def _():
+        for copy in copies:
+            copy.start()
+        for copy in copies:
+            copy.wait()
+
     first = lax.axis_index("lat") * slots + step * SUBLANES
-
     sub = lax.broadcasted_iota(jnp.int32, (SUBLANES, LANES), 0)
     lane = lax.broadcasted_iota(jnp.int32, (SUBLANES, LANES), 1)
     label = jnp.zeros((SUBLANES, LANES), jnp.int32)
     for s in range(SUBLANES):
         label = jnp.where(sub == s, azim_ref[first + s], label)
 
-    for t in range(tiles):
-        degree = (label + lane + t * LANES).astype(jnp.float32)
-        laplace = degree * (degree + 1.0)
-        den = [1.0 / (1.0 + cel_ref[m] * laplace) for m in range(levels)]
-        ref = rhs_refs[t]
-        x0 = [[ref[l * 2 + c] for c in range(2)] for l in range(levels)]
+    for group in range(0, tiles, 2):
+        ts = list(range(group, min(group + 2, tiles)))
+        parts = [(t, c) for t in ts for c in range(2)]
+        span = range(len(parts))
+
+        def mix(matrix, row, operand):
+            acc = [matrix[row, 0] * operand[0][i] for i in span]
+            for q in range(1, levels):
+                acc = [acc[i] + matrix[row, q] * operand[q][i] for i in span]
+            return acc
+
+        laplace = []
+        for t in ts:
+            degree = (label + lane + t * LANES).astype(jnp.float32)
+            laplace.append(degree * (degree + 1.0))
+        x0 = [[rhs_refs[t][l * 2 + c] for t, c in parts] for l in range(levels)]
         damped = []
         for m in range(levels):
-            acc = [fwd_ref[m, 0] * x0[0][c] for c in range(2)]
-            for l in range(1, levels):
-                acc = [acc[c] + fwd_ref[m, l] * x0[l][c] for c in range(2)]
-            damped.append([acc[c] * den[m] for c in range(2)])
+            modal = mix(fwd_ref, m, x0)
+            den = [1.0 / (1.0 + cel_ref[m] * lap) for lap in laplace]
+            damped.append([modal[i] * den[i // 2] for i in span])
         div = []
         for l in range(levels):
-            acc = [back_ref[l, 0] * damped[0][c] for c in range(2)]
-            for m in range(1, levels):
-                acc = [acc[c] + back_ref[l, m] * damped[m][c] for c in range(2)]
-            div.append(acc)
-            for c in range(2):
-                upd_ref[t, pl.ds((l * 2 + c) * SUBLANES, SUBLANES), :] = acc[c]
+            div.append(mix(back_ref, l, damped))
+            for i, (t, c) in enumerate(parts):
+                pad_ref[t, pl.ds((l * 2 + c) * pitch, SUBLANES), :] = div[l][i]
         for l in range(levels):
-            acc = [therm_ref[l, 0] * div[0][c] for c in range(2)]
-            for q in range(1, levels):
-                acc = [acc[c] + therm_ref[l, q] * div[q][c] for c in range(2)]
-            for c in range(2):
-                upd_ref[t, pl.ds(((levels + l) * 2 + c) * SUBLANES, SUBLANES), :] = (
-                    ref[(levels + l) * 2 + c] - acc[c]
-                )
-
-    solved = 4 * levels
-    rest = rows - solved
+            response = mix(therm_ref, l, div)
+            for i, (t, c) in enumerate(parts):
+                row = (levels + l) * 2 + c
+                pad_ref[t, pl.ds(row * pitch, SUBLANES), :] = rhs_refs[t][row] - response[i]
+
+    for t in range(tiles):
+        for row in range(4 * levels, rows):
+            pad_ref[t, pl.ds(row * pitch, SUBLANES), :] = rhs_refs[t][row]
+
     for s in range(SUBLANES):
         room = waves - azim_ref[first + s]
         pieces = []
         for t in range(tiles):
-            flat = rhs_refs[t].reshape(rows * SUBLANES, LANES)
-            parts = []
-            for c in range(2):
-                parts.append(
-                    upd_ref[t, pl.ds(c * SUBLANES + s, solved // 2, stride=2 * SUBLANES), :]
-                )
-                parts.append(
-                    flat[pl.ds((solved + c) * SUBLANES + s, rest // 2, stride=2 * SUBLANES), :]
-                )
-            piece = jnp.concatenate(parts, 0)
+            piece = jnp.concatenate(
+                [pad_ref[t, pl.ds(c * pitch + s, rows // 2, stride=2 * pitch), :] for c in range(2)],
+                0,
+            )
             k = lax.broadcasted_iota(jnp.int32, piece.shape, 1) + t * LANES
             pieces.append(jnp.where(k < room, piece, 0.0).astype(jnp.bfloat16))
         coeffs = jnp.concatenate(pieces, 1)
         product = lax.dot_general(
             polar_ref[s], coeffs, (((1,), (1,)), ((), ())), preferred_element_type=jnp.float32
         )
-        nat_ref[pl.ds((step * SUBLANES + s) * nlat, nlat), :] = product
+        nat_ref[pl.ds((step * SUBLANES + s) * apart, nlat), :] = product
 
     @pl.when(step == pl.num_programs(0) - 1)
     def _():
@@ -136,14 +151,22 @@
         low = lax.broadcasted_iota(jnp.int32, (slots, LANES), 1) < half
 
         def pair(p, carry):
-            a = nat_ref[pl.ds(arr_ref[2 * p], slots, stride=nlat), :]
-            b = nat_ref[pl.ds(arr_ref[2 * p + 1], slots, stride=nlat), :]
+            a = nat_ref[pl.ds(arr_ref[2 * p], slots, stride=apart), :]
+            b = nat_ref[pl.ds(arr_ref[2 * p + 1], slots, stride=apart), :]
             real = jnp.where(low, a, pltpu.roll(b, half, 1))
             imag = jnp.where(low, pltpu.roll(a, half, 1), b)
             out_ref[p] = jnp.concatenate([real, imag], 0).astype(jnp.bfloat16)
             return carry
 
         lax.fori_loop(0, nlat // 2, pair, 0, unroll=4)
+
+
+def row_pitch():
+    return SUBLANES + 1
+
+
+def slot_pitch(nlat):
+    return nlat + 4
 
 
 def legendre(rhs, azimuthal, arrangement, polar, forward, back, celerity, thermal):
@@ -151,7 +174,7 @@
     slots, nlat, waves = polar.shape
     rows = fields * levels * 2
     tiles = waves // LANES
-    smem = pl.BlockSpec(memory_space=pltpu.SMEM)
+    scalars = (azimuthal, arrangement, forward, back, celerity, thermal)
     flat = rhs.reshape(rows, slots, waves)
     rhs_specs = [
         pl.BlockSpec((rows, SUBLANES, LANES), functools.partial(lambda t, i: (0, i, t), t))
@@ -162,18 +185,20 @@
             legendre_kernel, levels=levels, slots=slots, nlat=nlat, waves=waves
         ),
         grid=(slots // SUBLANES,),
-        in_specs=[smem] * 6
+        in_specs=[pl.BlockSpec(memory_space=pltpu.HBM)] * len(scalars)
         + rhs_specs
         + [pl.BlockSpec((SUBLANES, nlat, waves), lambda i: (i, 0, 0))],
         out_specs=pl.BlockSpec((nlat // 2, 2 * slots, LANES), lambda i: (0, 0, 0)),
         out_shape=jax.ShapeDtypeStruct((nlat // 2, 2 * slots, LANES), jnp.bfloat16),
         scratch_shapes=[
-            pltpu.VMEM((slots * nlat, LANES), jnp.float32),
-            pltpu.VMEM((tiles, 4 * levels * SUBLANES, LANES), jnp.float32),
-        ],
-        compiler_params=pltpu.CompilerParams(vmem_limit_bytes=36 * 1024 * 1024),
+            pltpu.VMEM((slots * slot_pitch(nlat), LANES), jnp.float32),
+            pltpu.VMEM((tiles, rows * row_pitch(), LANES), jnp.float32),
+        ]
+        + [pltpu.SMEM(a.shape, a.dtype) for a in scalars]
+        + [pltpu.SemaphoreType.DMA((len(scalars),))],
+        compiler_params=pltpu.CompilerParams(vmem_limit_bytes=56 * 1024 * 1024),
         name="legendre",
-    )(azimuthal, arrangement, forward, back, celerity, thermal, *([flat] * tiles), polar)
+    )(*scalars, *([flat] * tiles), polar)
 
 
 def table_kernel(azim_ref, out_ref, *, slots, nlon):
@@ -211,10 +236,8 @@
     )(spread)
 
 
-def grid_kernel(x_ref, tab_ref, out_ref, lhs_ref, acc_ref, *, lat_dev):
+def grid_kernel(x_ref, tab_ref, out_ref, lhs_ref, *, fields, lat_dev):
     depth = tab_ref.shape[0]
-    tiles = tab_ref.shape[1] // LANES
-    half = LANES // 2
 
     @pl.when(pl.program_id(0) == 0)
     def _():
@@ -222,38 +245,35 @@
             block = x_ref[:, p].reshape(depth, LANES)
             lhs_ref[pl.ds(p * LANES, LANES), :] = block.T
 
+    half = LANES // 2
+    levels = half // fields
     product = jnp.dot(lhs_ref[...], tab_ref[...], preferred_element_type=jnp.float32)
-    for t in range(tiles):
-        acc_ref[t] = product[:, t * LANES : (t + 1) * LANES]
-
-    for t in range(tiles):
-        for i in range(half):
-            out_ref[i, :, t * LANES : (t + 1) * LANES] = acc_ref[
-                t, pl.ds(i, lat_dev, stride=half), :
-            ].astype(jnp.bfloat16)
-
-
-def grid_product(received, tab, lat_dev, block=512):
+    for r in range(lat_dev):
+        for f in range(fields):
+            row = r * half + f * levels
+            out_ref[f, r] = product[row : row + levels].astype(jnp.bfloat16)
+
+
+def grid_product(received, tab, lat_dev, fields, block=512):
     devices = received.shape[0]
     depth = tab.shape[0] * tab.shape[1]
     half = LANES // 2
+    levels = half // fields
     x = received.reshape(devices, lat_dev // 2, depth // devices, LANES)
-    return pl.pallas_call(
-        functools.partial(grid_kernel, lat_dev=lat_dev),
+    out = pl.pallas_call(
+        functools.partial(grid_kernel, fields=fields, lat_dev=lat_dev),
         grid=(NLON // block,),
         in_specs=[
             pl.BlockSpec(x.shape, lambda j: (0, 0, 0, 0)),
             pl.BlockSpec((depth, block), lambda j: (0, j)),
         ],
-        out_specs=pl.BlockSpec((half, lat_dev, block), lambda j: (0, 0, j)),
-        out_shape=jax.ShapeDtypeStruct((half, lat_dev, NLON), jnp.bfloat16),
-        scratch_shapes=[
-            pltpu.VMEM((lat_dev * half, depth), jnp.bfloat16),
-            pltpu.VMEM((block // LANES, lat_dev * half, LANES), jnp.float32),
-        ],
-        compiler_params=pltpu.CompilerParams(vmem_limit_bytes=24 * 1024 * 1024),
+        out_specs=pl.BlockSpec((fields, lat_dev, levels, block), lambda j: (0, 0, 0, j)),
+        out_shape=jax.ShapeDtypeStruct((fields, lat_dev, levels, NLON), jnp.bfloat16),
+        scratch_shapes=[pltpu.VMEM((lat_dev * half, depth), jnp.bfloat16)],
+        compiler_params=pltpu.CompilerParams(vmem_limit_bytes=48 * 1024 * 1024),
         name="grid_product",
     )(x, tab.reshape(depth, NLON))
+    return jnp.swapaxes(out, 1, 2)
 
 
 def per_device(rhs, azimuthal, arrangement, polar, forward, back, celerity, thermal):
@@ -265,8 +285,7 @@
     packed = packed.reshape(devices, lat_dev * slots, LANES)
     received = lax.all_to_all(packed, "lat", split_axis=0, concat_axis=0, tiled=True)
     tab = table(azimuthal, devices, slots)
-    grid_out = grid_product(received, tab, lat_dev)
-    return grid_out.reshape(fields, levels, lat_dev, NLON)
+    return grid_product(received, tab, lat_dev, fields)
 
 
 def solution(mesh):

time: 87 us -> 68.2 us (0.78)
  local copies, waits for them, and re-layouts: 16.8 us -> 2.96 us
  Pallas kernels: 35.4 us -> 30.4 us
    unnamed x20 -> x4, local copies, waits for them, and re-layouts: 13 us -> 2.75 us
    reshape x1 -> x0, local copies, waits for them, and re-layouts: 3.57 us -> none  [per_device(): return grid_out.reshape(fields, levels, lat_dev, NLON)]
    pallas_call x1, Pallas kernels: 11.5 us -> 8.81 us  [grid_product(): pl.pallas_call(functools.partial(grid_kernel, fields=fields, lat_dev=lat_...]
    pallas_call x1, Pallas kernels: 17.1 us -> 14.9 us  [legendre(): pl.pallas_call(functools.partial(legendre_kernel, levels=levels, slots=sl...]
  transfers between devices with their start and end apart: 1 -> 1, of which waited for: 1 -> 1; matrix products, arithmetic and copies ran while one was open for 0% -> 0% of each run, Pallas kernels for 8% -> 10%
where the time goes in v2:
time: 68.2 us; the launch traced here: 67.8 us
  Pallas kernels  30.4 us (45%)
  waiting for transfers between devices  27.9 us (41%)
  starting transfers between devices  6.53 us (10%)
  local copies, waits for them, and re-layouts  2.96 us (4%)
    all_to_all x1, waiting for transfers between devices, per_device(): lax.all_to_all(packed, 'lat', split_axis=0, concat_axis=0, tiled=True)  27.9 us
    pallas_call x1, Pallas kernels, legendre(): pl.pallas_call(functools.partial(legendre_kernel, levels=levels, slots=sl...  14.9 us
    pallas_call x1, Pallas kernels, grid_product(): pl.pallas_call(functools.partial(grid_kernel, fields=fields, lat_dev=lat_...  8.81 us
    pallas_call x1, Pallas kernels, table(): pl.pallas_call(functools.partial(table_kernel, slots=slots, nlon=NLON), g...  6.72 us
    all_to_all x1, starting transfers between devices, per_device(): lax.all_to_all(packed, 'lat', split_axis=0, concat_axis=0, tiled=True)  6.53 us
    unnamed x4, local copies, waits for them, and re-layouts  2.75 us
  transfers between devices with their start and end apart: 1, of which 1 were waited for; matrix products, arithmetic and copies ran while one was open for 0% of the time, Pallas kernels for 10%

profile of v2, /device:TPU:13, one launch (start us, length us, event | category | flops | bytes accessed | tf_op | source)
XLA Modules:
  0.0 67.8 jit_solution(17735781246554450585)
XLA Ops:
  0.0 0.0 copy-start.1
  0.0 14.9 %legendre.1 = bf16[80,80,128]{2,1,0:T(8,128)(2,1)} custom-call(s32[640]{0:T(1024)} %azim_hbm.1, s32[160]{0:T(256)} %arr_hbm.1, f32[8,8]{1,0:T(8,128)} %fwd_hbm.1, f32[8,8]{1,0:T(8,128)} %back_hbm.1, f32[8]{0:T(128)} %cel_hbm.1, f32[8,8]{1,0:T(8,128)} %therm_hbm.1, f32[128,40,640]{2,1,0:T(8,128)} %bitcast.7, f32[128,40,640]{2,1,0:T(8,128)} %bitcast.8, ...), custom_call_target="tpu_custom_call" | custom-call | tf_op jit(solution)/shard_map/legendre/pallas_call | solution.py:183
  14.9 6.5 %all-to-all-start = ((bf16[16,400,128]{2,1,0:T(8,128)(2,1)}), bf16[16,400,128]{2,1,0:T(8,128)(2,1)S(1)}, u32[]{:S(2)}, u32[]{:S(2)}) async-start(bf16[16,400,128]{2,1,0:T(8,128)(2,1)} %bitcast.12), calls=%async_computation | async-start | bytes 3276800 | tf_op jit(solution)/shard_map/all_to_all | solution.py:286
  21.4 0.0 copy-done.1
  21.4 0.1 broadcast_in_dim.7
  21.5 0.1 broadcast_in_dim.8.azim_ref
  21.6 6.7 %table.1 = bf16[16,80,2560]{2,1,0:T(8,128)(2,1)S(1)} custom-call(s32[16,40,128]{2,1,0:T(8,128)S(1)} %broadcast_in_dim.8.azim_ref), custom_call_target="tpu_custom_call" | custom-call | tf_op jit(solution)/shard_map/table/pallas_call | solution.py:228
  28.4 0.0 copy-start
  28.4 2.7 %copy-done = bf16[16,80,2560]{2,1,0:T(8,128)(2,1)} copy-done((bf16[16,80,2560]{2,1,0:T(8,128)(2,1)}, bf16[16,80,2560]{2,1,0:T(8,128)(2,1)S(1)}, u32[]{:S(2)}) %copy-start) | copy-done | bytes 6553624
  31.1 27.9 %all-to-all-done = bf16[16,400,128]{2,1,0:T(8,128)(2,1)S(1)} async-done(((bf16[16,400,128]{2,1,0:T(8,128)(2,1)}), bf16[16,400,128]{2,1,0:T(8,128)(2,1)S(1)}, u32[]{:S(2)}, u32[]{:S(2)}) %all-to-all-start) | async-done | bytes 1638432 | tf_op jit(solution)/shard_map/all_to_all | solution.py:286
  59.0 8.8 %grid_product.1 = bf16[8,10,8,2560]{3,2,1,0:T(8,128)(2,1)} custom-call(bf16[16,5,80,128]{3,2,1,0:T(8,128)(2,1)S(1)} %bitcast.6, bf16[1280,2560]{1,0:T(8,128)(2,1)} %bitcast.5), custom_call_target="tpu_custom_call" | custom-call | tf_op jit(solution)/shard_map/grid_product/pallas_call | solution.py:263
Async XLA Ops:
  0.0 21.4 %copy-start.1 = (s32[640]{0:T(1024)S(1)}, s32[640]{0:T(1024)}, u32[]{:S(2)}) copy-start(s32[640]{0:T(1024)} %azim_hbm.1) | copy-start | bytes 7684
  14.9 44.1 %all-to-all-start = ((bf16[16,400,128]{2,1,0:T(8,128)(2,1)}), bf16[16,400,128]{2,1,0:T(8,128)(2,1)S(1)}, u32[]{:S(2)}, u32[]{:S(2)}) async-start(bf16[16,400,128]{2,1,0:T(8,128)(2,1)} %bitcast.12), calls=%async_computation | async-start | bytes 3276800 | tf_op jit(solution)/shard_map/all_to_all | solution.py:286
  28.4 2.8 %copy-start = (bf16[16,80,2560]{2,1,0:T(8,128)(2,1)}, bf16[16,80,2560]{2,1,0:T(8,128)(2,1)S(1)}, u32[]{:S(2)}) copy-start(bf16[16,80,2560]{2,1,0:T(8,128)(2,1)S(1)} %table.1) | copy-start | bytes 19660804

commit v3 on v2

--- a/solution.py
+++ b/solution.py
@@ -9,6 +9,7 @@
 NLON = 2560
 LANES = 128
 SUBLANES = 8
+GROUP = 2
 full_circle_radians = 6.283185307179586
 
 
@@ -62,29 +63,17 @@
 
 
 def legendre_kernel(
-    azim_hbm, arr_hbm, fwd_hbm, back_hbm, cel_hbm, therm_hbm, *refs, levels, slots, nlat, waves
+    azim_ref, arr_ref, fwd_ref, back_ref, cel_ref, therm_ref, rhs_ref, polar_ref, out_ref,
+    nat_ref, pad_ref, *, levels, slots, nlat, waves
 ):
     tiles = waves // LANES
-    rhs_refs = refs[:tiles]
-    polar_ref, out_ref, nat_ref, pad_ref = refs[tiles : tiles + 4]
-    scalars, sems = refs[tiles + 4 : -1], refs[-1]
-    azim_ref, arr_ref, fwd_ref, back_ref, cel_ref, therm_ref = scalars
-    sources = (azim_hbm, arr_hbm, fwd_hbm, back_hbm, cel_hbm, therm_hbm)
-    copies = [
-        pltpu.make_async_copy(src, dst, sems.at[i])
-        for i, (src, dst) in enumerate(zip(sources, scalars))
-    ]
-    rows = rhs_refs[0].shape[0]
+    rows = rhs_ref.shape[0]
     pitch = row_pitch()
     apart = slot_pitch(nlat)
     step = pl.program_id(0)
 
-    @pl.when(step == 0)
-    def _():
-        for copy in copies:
-            copy.start()
-        for copy in copies:
-            copy.wait()
+    def rhs(row, t):
+        return rhs_ref[row, :, t * LANES : (t + 1) * LANES]
 
     first = lax.axis_index("lat") * slots + step * SUBLANES
     sub = lax.broadcasted_iota(jnp.int32, (SUBLANES, LANES), 0)
@@ -93,8 +82,8 @@
     for s in range(SUBLANES):
         label = jnp.where(sub == s, azim_ref[first + s], label)
 
-    for group in range(0, tiles, 2):
-        ts = list(range(group, min(group + 2, tiles)))
+    for group in range(0, tiles, GROUP):
+        ts = list(range(group, min(group + GROUP, tiles)))
         parts = [(t, c) for t in ts for c in range(2)]
         span = range(len(parts))
 
@@ -108,7 +97,7 @@
         for t in ts:
             degree = (label + lane + t * LANES).astype(jnp.float32)
             laplace.append(degree * (degree + 1.0))
-        x0 = [[rhs_refs[t][l * 2 + c] for t, c in parts] for l in range(levels)]
+        x0 = [[rhs(l * 2 + c, t) for t, c in parts] for l in range(levels)]
         damped = []
         for m in range(levels):
             modal = mix(fwd_ref, m, x0)
@@ -123,11 +112,11 @@
             response = mix(therm_ref, l, div)
             for i, (t, c) in enumerate(parts):
                 row = (levels + l) * 2 + c
-                pad_ref[t, pl.ds(row * pitch, SUBLANES), :] = rhs_refs[t][row] - response[i]
+                pad_ref[t, pl.ds(row * pitch, SUBLANES), :] = rhs(row, t) - response[i]
 
     for t in range(tiles):
         for row in range(4 * levels, rows):
-            pad_ref[t, pl.ds(row * pitch, SUBLANES), :] = rhs_refs[t][row]
+            pad_ref[t, pl.ds(row * pitch, SUBLANES), :] = rhs(row, t)
 
     for s in range(SUBLANES):
         room = waves - azim_ref[first + s]
@@ -143,22 +132,19 @@
         product = lax.dot_general(
             polar_ref[s], coeffs, (((1,), (1,)), ((), ())), preferred_element_type=jnp.float32
         )
-        nat_ref[pl.ds((step * SUBLANES + s) * apart, nlat), :] = product
-
-    @pl.when(step == pl.num_programs(0) - 1)
-    def _():
-        half = LANES // 2
-        low = lax.broadcasted_iota(jnp.int32, (slots, LANES), 1) < half
-
-        def pair(p, carry):
-            a = nat_ref[pl.ds(arr_ref[2 * p], slots, stride=apart), :]
-            b = nat_ref[pl.ds(arr_ref[2 * p + 1], slots, stride=apart), :]
-            real = jnp.where(low, a, pltpu.roll(b, half, 1))
-            imag = jnp.where(low, pltpu.roll(a, half, 1), b)
-            out_ref[p] = jnp.concatenate([real, imag], 0).astype(jnp.bfloat16)
-            return carry
-
-        lax.fori_loop(0, nlat // 2, pair, 0, unroll=4)
+        nat_ref[pl.ds(s * apart, nlat), :] = product
+
+    half = LANES // 2
+    low = lane < half
+    pairs = out_ref.shape[1] // (2 * SUBLANES)
+    for p in range(nlat // 2):
+        a = nat_ref[pl.ds(arr_ref[2 * p], SUBLANES, stride=apart), :]
+        b = nat_ref[pl.ds(arr_ref[2 * p + 1], SUBLANES, stride=apart), :]
+        real = jnp.where(low, a, pltpu.roll(b, half, 1))
+        imag = jnp.where(low, pltpu.roll(a, half, 1), b)
+        out_ref[p // pairs, pl.ds(p % pairs * 2 * SUBLANES, 2 * SUBLANES), :] = jnp.concatenate(
+            [real, imag], 0
+        ).astype(jnp.bfloat16)
 
 
 def row_pitch():
@@ -174,31 +160,29 @@
     slots, nlat, waves = polar.shape
     rows = fields * levels * 2
     tiles = waves // LANES
+    devices = lax.axis_size("lat")
+    steps = slots // SUBLANES
+    depth = nlat // devices * SUBLANES
     scalars = (azimuthal, arrangement, forward, back, celerity, thermal)
-    flat = rhs.reshape(rows, slots, waves)
-    rhs_specs = [
-        pl.BlockSpec((rows, SUBLANES, LANES), functools.partial(lambda t, i: (0, i, t), t))
-        for t in range(tiles)
-    ]
     return pl.pallas_call(
         functools.partial(
             legendre_kernel, levels=levels, slots=slots, nlat=nlat, waves=waves
         ),
-        grid=(slots // SUBLANES,),
-        in_specs=[pl.BlockSpec(memory_space=pltpu.HBM)] * len(scalars)
-        + rhs_specs
-        + [pl.BlockSpec((SUBLANES, nlat, waves), lambda i: (i, 0, 0))],
-        out_specs=pl.BlockSpec((nlat // 2, 2 * slots, LANES), lambda i: (0, 0, 0)),
-        out_shape=jax.ShapeDtypeStruct((nlat // 2, 2 * slots, LANES), jnp.bfloat16),
+        grid=(steps,),
+        in_specs=[pl.BlockSpec(memory_space=pltpu.SMEM)] * len(scalars)
+        + [
+            pl.BlockSpec((rows, SUBLANES, waves), lambda i: (0, i, 0)),
+            pl.BlockSpec((SUBLANES, nlat, waves), lambda i: (i, 0, 0)),
+        ],
+        out_specs=pl.BlockSpec((devices, None, depth, LANES), lambda i: (0, i, 0, 0)),
+        out_shape=jax.ShapeDtypeStruct((devices, steps, depth, LANES), jnp.bfloat16),
         scratch_shapes=[
-            pltpu.VMEM((slots * slot_pitch(nlat), LANES), jnp.float32),
+            pltpu.VMEM((SUBLANES * slot_pitch(nlat), LANES), jnp.float32),
             pltpu.VMEM((tiles, rows * row_pitch(), LANES), jnp.float32),
-        ]
-        + [pltpu.SMEM(a.shape, a.dtype) for a in scalars]
-        + [pltpu.SemaphoreType.DMA((len(scalars),))],
-        compiler_params=pltpu.CompilerParams(vmem_limit_bytes=56 * 1024 * 1024),
+        ],
+        compiler_params=pltpu.CompilerParams(vmem_limit_bytes=60 * 1024 * 1024),
         name="legendre",
-    )(*scalars, *([flat] * tiles), polar)
+    )(*scalars, rhs.reshape(rows, slots, waves), polar)
 
 
 def table_kernel(azim_ref, out_ref, *, slots, nlon):
@@ -218,9 +202,10 @@
         sc = sin_coarse[:, b : b + 1]
         real = cos_fine * cc - sin_fine * sc
         imag = -(sin_fine * cc + cos_fine * sc)
-        out_ref[0, :, b * LANES : (b + 1) * LANES] = jnp.concatenate([real, imag], 0).astype(
-            jnp.bfloat16
-        )
+        rows = []
+        for s in range(0, slots, SUBLANES):
+            rows += [real[s : s + SUBLANES], imag[s : s + SUBLANES]]
+        out_ref[0, :, b * LANES : (b + 1) * LANES] = jnp.concatenate(rows, 0).astype(jnp.bfloat16)
 
 
 def table(azimuthal, devices, slots):
@@ -242,7 +227,7 @@
     @pl.when(pl.program_id(0) == 0)
     def _():
         for p in range(lat_dev // 2):
-            block = x_ref[:, p].reshape(depth, LANES)
+            block = x_ref[:, :, p].reshape(depth, LANES)
             lhs_ref[pl.ds(p * LANES, LANES), :] = block.T
 
     half = LANES // 2
@@ -255,16 +240,16 @@
 
 
 def grid_product(received, tab, lat_dev, fields, block=512):
-    devices = received.shape[0]
+    devices, steps = received.shape[:2]
     depth = tab.shape[0] * tab.shape[1]
     half = LANES // 2
     levels = half // fields
-    x = received.reshape(devices, lat_dev // 2, depth // devices, LANES)
+    x = received.reshape(devices, steps, lat_dev // 2, 2 * SUBLANES, LANES)
     out = pl.pallas_call(
         functools.partial(grid_kernel, fields=fields, lat_dev=lat_dev),
         grid=(NLON // block,),
         in_specs=[
-            pl.BlockSpec(x.shape, lambda j: (0, 0, 0, 0)),
+            pl.BlockSpec(memory_space=pltpu.VMEM),
             pl.BlockSpec((depth, block), lambda j: (0, j)),
         ],
         out_specs=pl.BlockSpec((fields, lat_dev, levels, block), lambda j: (0, 0, 0, j)),
@@ -282,7 +267,6 @@
     devices = lax.axis_size("lat")
     lat_dev = nlat // devices
     packed = legendre(rhs, azimuthal, arrangement, polar, forward, back, celerity, thermal)
-    packed = packed.reshape(devices, lat_dev * slots, LANES)
     received = lax.all_to_all(packed, "lat", split_axis=0, concat_axis=0, tiled=True)
     tab = table(azimuthal, devices, slots)
     return grid_product(received, tab, lat_dev, fields)

time: 68.2 us -> 65.4 us (0.959)
  Pallas kernels: 30.4 us -> 27.7 us
    pallas_call x1, Pallas kernels: 14.9 us -> 12.2 us  [legendre(): pl.pallas_call(functools.partial(legendre_kernel, levels=levels, slots=sl...]
where the time goes in v3:
time: 65.4 us; the launch traced here: 65.1 us
  waiting for transfers between devices  27.9 us (43%)
  Pallas kernels  27.7 us (42%)
  starting transfers between devices  6.52 us (10%)
  local copies, waits for them, and re-layouts  2.96 us (5%)
    all_to_all x1, waiting for transfers between devices, per_device(): lax.all_to_all(packed, 'lat', split_axis=0, concat_axis=0, tiled=True)  27.9 us
    pallas_call x1, Pallas kernels, legendre(): pl.pallas_call(functools.partial(legendre_kernel, levels=levels, slots=sl...  12.2 us
    pallas_call x1, Pallas kernels, grid_product(): pl.pallas_call(functools.partial(grid_kernel, fields=fields, lat_dev=lat_...  8.81 us
    pallas_call x1, Pallas kernels, table(): pl.pallas_call(functools.partial(table_kernel, slots=slots, nlon=NLON), g...  6.72 us
    all_to_all x1, starting transfers between devices, per_device(): lax.all_to_all(packed, 'lat', split_axis=0, concat_axis=0, tiled=True)  6.52 us
    unnamed x4, local copies, waits for them, and re-layouts  2.75 us
  transfers between devices with their start and end apart: 1, of which 1 were waited for; matrix products, arithmetic and copies ran while one was open for 0% of the time, Pallas kernels for 10%

profile of v3, /device:TPU:13, one launch (start us, length us, event | category | flops | bytes accessed | tf_op | source)
XLA Modules:
  0.0 65.1 jit_solution(7451333755260208712)
XLA Ops:
  0.0 0.0 copy-start.1
  0.0 12.2 %legendre.1 = bf16[16,5,80,128]{3,2,1,0:T(8,128)(2,1)} custom-call(s32[640]{0:T(1024)} %azim_ref.1, s32[160]{0:T(256)} %arr_ref.1, f32[8,8]{1,0:T(8,128)} %fwd_ref.1, f32[8,8]{1,0:T(8,128)} %back_ref.1, f32[8]{0:T(128)} %cel_ref.1, f32[8,8]{1,0:T(8,128)} %therm_ref.1, f32[128,40,640]{2,1,0:T(8,128)} %bitcast.6, bf16[40,160,640]{2,1,0:T(8,128)(2,1)} %polar_ref.1), custom_call_target="tpu_custom_call" | custom-call | tf_op jit(solution)/shard_map/legendre/pallas_call | solution.py:167
  12.2 6.5 %all-to-all-start = ((bf16[16,5,80,128]{3,2,1,0:T(8,128)(2,1)}), bf16[16,5,80,128]{3,2,1,0:T(8,128)(2,1)S(1)}, u32[]{:S(2)}, u32[]{:S(2)}) async-start(bf16[16,5,80,128]{3,2,1,0:T(8,128)(2,1)} %legendre.1), calls=%async_computation | async-start | bytes 3276800 | tf_op jit(solution)/shard_map/all_to_all | solution.py:270
  18.7 0.0 copy-done.1
  18.7 0.1 broadcast_in_dim.7
  18.8 0.1 broadcast_in_dim.8.azim_ref
  19.0 6.7 %table.1 = bf16[16,80,2560]{2,1,0:T(8,128)(2,1)S(1)} custom-call(s32[16,40,128]{2,1,0:T(8,128)S(1)} %broadcast_in_dim.8.azim_ref), custom_call_target="tpu_custom_call" | custom-call | tf_op jit(solution)/shard_map/table/pallas_call | solution.py:213
  25.7 0.0 copy-start
  25.7 2.7 %copy-done = bf16[16,80,2560]{2,1,0:T(8,128)(2,1)} copy-done((bf16[16,80,2560]{2,1,0:T(8,128)(2,1)}, bf16[16,80,2560]{2,1,0:T(8,128)(2,1)S(1)}, u32[]{:S(2)}) %copy-start) | copy-done | bytes 6553624
  28.4 27.9 %all-to-all-done = bf16[16,5,80,128]{3,2,1,0:T(8,128)(2,1)S(1)} async-done(((bf16[16,5,80,128]{3,2,1,0:T(8,128)(2,1)}), bf16[16,5,80,128]{3,2,1,0:T(8,128)(2,1)S(1)}, u32[]{:S(2)}, u32[]{:S(2)}) %all-to-all-start) | async-done | bytes 1638432 | tf_op jit(solution)/shard_map/all_to_all | solution.py:270
  56.3 8.8 %grid_product.1 = bf16[8,10,8,2560]{3,2,1,0:T(8,128)(2,1)} custom-call(bf16[16,5,5,16,128]{4,3,2,1,0:T(8,128)(2,1)S(1)} %bitcast.5, bf16[1280,2560]{1,0:T(8,128)(2,1)} %bitcast.4), custom_call_target="tpu_custom_call" | custom-call | tf_op jit(solution)/shard_map/grid_product/pallas_call | solution.py:248
Async XLA Ops:
  0.0 18.7 %copy-start.1 = (s32[640]{0:T(1024)S(1)}, s32[640]{0:T(1024)}, u32[]{:S(2)}) copy-start(s32[640]{0:T(1024)} %azim_ref.1) | copy-start | bytes 7684
  12.2 44.1 %all-to-all-start = ((bf16[16,5,80,128]{3,2,1,0:T(8,128)(2,1)}), bf16[16,5,80,128]{3,2,1,0:T(8,128)(2,1)S(1)}, u32[]{:S(2)}, u32[]{:S(2)}) async-start(bf16[16,5,80,128]{3,2,1,0:T(8,128)(2,1)} %legendre.1), calls=%async_computation | async-start | bytes 3276800 | tf_op jit(solution)/shard_map/all_to_all | solution.py:270
  25.7 2.8 %copy-start = (bf16[16,80,2560]{2,1,0:T(8,128)(2,1)}, bf16[16,80,2560]{2,1,0:T(8,128)(2,1)S(1)}, u32[]{:S(2)}) copy-start(bf16[16,80,2560]{2,1,0:T(8,128)(2,1)S(1)} %table.1) | copy-start | bytes 19660804

commit v4 on v3

--- a/solution.py
+++ b/solution.py
@@ -185,10 +185,10 @@
     )(*scalars, rhs.reshape(rows, slots, waves), polar)
 
 
-def table_kernel(azim_ref, out_ref, *, slots, nlon):
+def table_kernel(azim_ref, cos_ref, sin_ref, *, nlon):
     blocks = nlon // LANES
-    m = azim_ref[0]
-    lane = lax.broadcasted_iota(jnp.int32, (slots, LANES), 1)
+    m = azim_ref[...]
+    lane = lax.broadcasted_iota(jnp.int32, m.shape, 1)
     unit = full_circle_radians / nlon
     fine = ((m * lane) % nlon).astype(jnp.float32) * unit
     coarse = ((m * lane) % blocks).astype(jnp.float32) * (unit * LANES)
@@ -197,67 +197,130 @@
     sin_fine = weight * jnp.sin(fine)
     cos_coarse = jnp.cos(coarse)
     sin_coarse = jnp.sin(coarse)
-    for b in range(blocks):
+    for b in range(blocks // 2 + 1):
         cc = cos_coarse[:, b : b + 1]
         sc = sin_coarse[:, b : b + 1]
-        real = cos_fine * cc - sin_fine * sc
-        imag = -(sin_fine * cc + cos_fine * sc)
-        rows = []
-        for s in range(0, slots, SUBLANES):
-            rows += [real[s : s + SUBLANES], imag[s : s + SUBLANES]]
-        out_ref[0, :, b * LANES : (b + 1) * LANES] = jnp.concatenate(rows, 0).astype(jnp.bfloat16)
-
-
-def table(azimuthal, devices, slots):
-    spread = jnp.broadcast_to(azimuthal.reshape(devices, slots, 1), (devices, slots, LANES))
+        at = slice(b * LANES, (b + 1) * LANES)
+        cos_ref[:, at] = (cos_fine * cc - sin_fine * sc).astype(jnp.bfloat16)
+        if b < blocks // 2:
+            sin_ref[:, at] = (-(sin_fine * cc + cos_fine * sc)).astype(jnp.bfloat16)
+
+
+def table(azimuthal, rows):
+    count = azimuthal.shape[0]
+    half = NLON // 2
+    spread = jnp.broadcast_to(azimuthal[:, None], (count, LANES))
     return pl.pallas_call(
-        functools.partial(table_kernel, slots=slots, nlon=NLON),
-        grid=(devices,),
-        in_specs=[pl.BlockSpec((1, slots, LANES), lambda d: (d, 0, 0))],
-        out_specs=pl.BlockSpec((1, 2 * slots, NLON), lambda d: (d, 0, 0)),
-        out_shape=jax.ShapeDtypeStruct((devices, 2 * slots, NLON), jnp.bfloat16),
+        functools.partial(table_kernel, nlon=NLON),
+        grid=(count // rows,),
+        in_specs=[pl.BlockSpec((rows, LANES), lambda d: (d, 0))],
+        out_specs=[
+            pl.BlockSpec((rows, half + LANES), lambda d: (d, 0)),
+            pl.BlockSpec((rows, half), lambda d: (d, 0)),
+        ],
+        out_shape=[
+            jax.ShapeDtypeStruct((count, half + LANES), jnp.bfloat16),
+            jax.ShapeDtypeStruct((count, half), jnp.bfloat16),
+        ],
         compiler_params=pltpu.CompilerParams(vmem_limit_bytes=16 * 1024 * 1024),
         name="table",
     )(spread)
 
 
-def grid_kernel(x_ref, tab_ref, out_ref, lhs_ref, *, fields, lat_dev):
-    depth = tab_ref.shape[0]
-
-    @pl.when(pl.program_id(0) == 0)
-    def _():
-        for p in range(lat_dev // 2):
-            block = x_ref[:, :, p].reshape(depth, LANES)
-            lhs_ref[pl.ds(p * LANES, LANES), :] = block.T
-
+def grid_kernel(
+    x_ref, cos_hbm, sin_hbm, out_hbm, cos_ref, sin_ref, real_ref, imag_ref, out_ref,
+    cos_sem, sin_sem, out_sem, *, fields, lat_dev, block,
+):
+    depth, width = sin_ref.shape
+    nlon = 2 * width
     half = LANES // 2
     levels = half // fields
-    product = jnp.dot(lhs_ref[...], tab_ref[...], preferred_element_type=jnp.float32)
-    for r in range(lat_dev):
-        for f in range(fields):
-            row = r * half + f * levels
-            out_ref[f, r] = product[row : row + levels].astype(jnp.bfloat16)
-
-
-def grid_product(received, tab, lat_dev, fields, block=512):
+    order = list(range(width // block))[::-1]
+
+    def span(i):
+        return pl.ds(i * block, block)
+
+    tail = pl.ds(width, LANES)
+    ends = pltpu.make_async_copy(
+        cos_hbm.at[:, tail], cos_ref.at[:, tail], cos_sem.at[len(order)]
+    )
+    loads = {}
+    ends.start()
+    for i in order:
+        loads[i] = [
+            pltpu.make_async_copy(cos_hbm.at[:, span(i)], cos_ref.at[:, span(i)], cos_sem.at[i]),
+            pltpu.make_async_copy(sin_hbm.at[:, span(i)], sin_ref.at[:, span(i)], sin_sem.at[i]),
+        ]
+        for copy in loads[i]:
+            copy.start()
+
+    for p in range(lat_dev // 2):
+        rows = x_ref[:, :, p].astype(jnp.float32)
+        for c, ref in enumerate((real_ref, imag_ref)):
+            part = rows[:, :, c * SUBLANES : (c + 1) * SUBLANES].reshape(depth, LANES)
+            ref[pl.ds(p * LANES, LANES), :] = part.astype(jnp.bfloat16).T
+
+    lane = lax.broadcasted_iota(jnp.int32, (lat_dev * half, LANES), 1)
+    mirror = (LANES - lane) % LANES
+    ends.wait()
+    after = jnp.dot(real_ref[...], cos_ref[:, tail], preferred_element_type=jnp.float32)
+    stores = []
+    for n, i in enumerate(order):
+        for copy in loads[i]:
+            copy.wait()
+        even = jnp.dot(real_ref[...], cos_ref[:, span(i)], preferred_element_type=jnp.float32)
+        odd = jnp.dot(imag_ref[...], sin_ref[:, span(i)], preferred_element_type=jnp.float32)
+        near = even + odd
+        far = even - odd
+        tiles = block // LANES
+        parts = [far[:, t * LANES : (t + 1) * LANES] for t in range(tiles)] + [after]
+        turned = [
+            jnp.where(lane == 0, parts[t + 1], jnp.take_along_axis(parts[t], mirror, axis=1))
+            for t in range(tiles)
+        ]
+        after = parts[0]
+        for q, value in enumerate((near, jnp.concatenate(turned[::-1], 1))):
+            for r in range(lat_dev):
+                for f in range(fields):
+                    row = r * half + f * levels
+                    out_ref[n, q, f, r] = value[row : row + levels].astype(jnp.bfloat16)
+            start = i * block if q == 0 else nlon - (i + 1) * block
+            stores.append(
+                pltpu.make_async_copy(
+                    out_ref.at[n, q], out_hbm.at[:, :, :, pl.ds(start, block)], out_sem.at[n, q]
+                )
+            )
+            stores[-1].start()
+    for copy in stores:
+        copy.wait()
+
+
+def grid_product(received, cos, sin, lat_dev, fields, block=256):
     devices, steps = received.shape[:2]
-    depth = tab.shape[0] * tab.shape[1]
+    depth, width = sin.shape
     half = LANES // 2
     levels = half // fields
+    count = width // block
     x = received.reshape(devices, steps, lat_dev // 2, 2 * SUBLANES, LANES)
+    hbm = pl.BlockSpec(memory_space=pltpu.HBM)
     out = pl.pallas_call(
-        functools.partial(grid_kernel, fields=fields, lat_dev=lat_dev),
-        grid=(NLON // block,),
-        in_specs=[
-            pl.BlockSpec(memory_space=pltpu.VMEM),
-            pl.BlockSpec((depth, block), lambda j: (0, j)),
-        ],
-        out_specs=pl.BlockSpec((fields, lat_dev, levels, block), lambda j: (0, 0, 0, j)),
-        out_shape=jax.ShapeDtypeStruct((fields, lat_dev, levels, NLON), jnp.bfloat16),
-        scratch_shapes=[pltpu.VMEM((lat_dev * half, depth), jnp.bfloat16)],
-        compiler_params=pltpu.CompilerParams(vmem_limit_bytes=48 * 1024 * 1024),
+        functools.partial(grid_kernel, fields=fields, lat_dev=lat_dev, block=block),
+        in_specs=[pl.BlockSpec(memory_space=pltpu.VMEM), hbm, hbm],
+        out_specs=hbm,
+        out_shape=jax.ShapeDtypeStruct((fields, lat_dev, levels, 2 * width), jnp.bfloat16),
+        scratch_shapes=[
+            pltpu.VMEM(cos.shape, jnp.bfloat16),
+            pltpu.VMEM(sin.shape, jnp.bfloat16),
+            pltpu.VMEM((lat_dev * half, depth), jnp.bfloat16),
+            pltpu.VMEM((lat_dev * half, depth), jnp.bfloat16),
+            pltpu.VMEM((count, 2, fields, lat_dev, levels, block), jnp.bfloat16),
+            pltpu.SemaphoreType.DMA((count + 1,)),
+            pltpu.SemaphoreType.DMA((count,)),
+            pltpu.SemaphoreType.DMA((count, 2)),
+        ],
+        compiler_params=pltpu.CompilerParams(vmem_limit_bytes=40 * 1024 * 1024),
         name="grid_product",
-    )(x, tab.reshape(depth, NLON))
+    )(x, *(pltpu.with_memory_space_constraint(a, pltpu.HBM) for a in (cos, sin)))
     return jnp.swapaxes(out, 1, 2)
 
 
@@ -268,8 +331,8 @@
     lat_dev = nlat // devices
     packed = legendre(rhs, azimuthal, arrangement, polar, forward, back, celerity, thermal)
     received = lax.all_to_all(packed, "lat", split_axis=0, concat_axis=0, tiled=True)
-    tab = table(azimuthal, devices, slots)
-    return grid_product(received, tab, lat_dev, fields)
+    cos, sin = table(azimuthal, 2 * slots)
+    return grid_product(received, cos, sin, lat_dev, fields)
 
 
 def solution(mesh):

time: 65.4 us -> 62.9 us (0.962)
  Pallas kernels: 27.7 us -> 23.1 us
  waiting for transfers between devices: 27.9 us -> 30.4 us
    pallas_call x1, Pallas kernels: 8.81 us -> 6.24 us  [grid_product(): pl.pallas_call(functools.partial(grid_kernel, fields=fields, lat_dev=lat_...]
    all_to_all x1, waiting for transfers between devices: 27.9 us -> 30.4 us  [per_device(): lax.all_to_all(packed, 'lat', split_axis=0, concat_axis=0, tiled=True)]
    pallas_call x1, Pallas kernels: 6.72 us -> 4.63 us  [table(): pl.pallas_call(functools.partial(table_kernel, nlon=NLON), grid=(count //...]
    unnamed x4 -> x6, local copies, waits for them, and re-layouts: 2.75 us -> 2.41 us
  transfers between devices with their start and end apart: 1 -> 1, of which waited for: 1 -> 1; matrix products, arithmetic and copies ran while one was open for 0% -> 0% of each run, Pallas kernels for 10% -> 7%
where the time goes in v4:
time: 62.9 us; the launch traced here: 62.7 us
  waiting for transfers between devices  30.4 us (48%)
  Pallas kernels  23.1 us (37%)
  starting transfers between devices  6.65 us (11%)
  local copies, waits for them, and re-layouts  2.54 us (4%)
    all_to_all x1, waiting for transfers between devices, per_device(): lax.all_to_all(packed, 'lat', split_axis=0, concat_axis=0, tiled=True)  30.4 us
    pallas_call x1, Pallas kernels, legendre(): pl.pallas_call(functools.partial(legendre_kernel, levels=levels, slots=sl...  12.2 us
    all_to_all x1, starting transfers between devices, per_device(): lax.all_to_all(packed, 'lat', split_axis=0, concat_axis=0, tiled=True)  6.65 us
    pallas_call x1, Pallas kernels, grid_product(): pl.pallas_call(functools.partial(grid_kernel, fields=fields, lat_dev=lat_...  6.24 us
    pallas_call x1, Pallas kernels, table(): pl.pallas_call(functools.partial(table_kernel, nlon=NLON), grid=(count //...  4.63 us
    unnamed x6, local copies, waits for them, and re-layouts  2.41 us
  transfers between devices with their start and end apart: 1, of which 1 were waited for; matrix products, arithmetic and copies ran while one was open for 0% of the time, Pallas kernels for 7%

profile of v4, /device:TPU:13, one launch (start us, length us, event | category | flops | bytes accessed | tf_op | source)
XLA Modules:
  0.0 62.7 jit_solution(9199360703686099110)
XLA Ops:
  0.0 12.2 %legendre.1 = bf16[16,5,80,128]{3,2,1,0:T(8,128)(2,1)} custom-call(s32[640]{0:T(1024)} %azim_ref.1, s32[160]{0:T(256)} %arr_ref.1, f32[8,8]{1,0:T(8,128)} %fwd_ref.1, f32[8,8]{1,0:T(8,128)} %back_ref.1, f32[8]{0:T(128)} %cel_ref.1, f32[8,8]{1,0:T(8,128)} %therm_ref.1, f32[128,40,640]{2,1,0:T(8,128)} %bitcast.4, bf16[40,160,640]{2,1,0:T(8,128)(2,1)} %polar_ref.1), custom_call_target="tpu_custom_call" | custom-call | tf_op jit(solution)/shard_map/legendre/pallas_call | solution.py:167
  12.2 0.0 copy-start.2
  12.2 6.7 %all-to-all-start = ((bf16[16,5,80,128]{3,2,1,0:T(8,128)(2,1)}), bf16[16,5,80,128]{3,2,1,0:T(8,128)(2,1)S(1)}, u32[]{:S(2)}, u32[]{:S(2)}) async-start(bf16[16,5,80,128]{3,2,1,0:T(8,128)(2,1)} %legendre.1), calls=%async_computation | async-start | bytes 3276800 | tf_op jit(solution)/shard_map/all_to_all | solution.py:333
  18.8 0.0 copy-done.2
  18.8 0.1 broadcast_in_dim.2.azim_ref
  19.0 4.6 %table.1 = (bf16[640,1408]{1,0:T(8,128)(2,1)S(1)}, bf16[640,1280]{1,0:T(8,128)(2,1)S(1)}) custom-call(s32[640,128]{1,0:T(8,128)S(1)} %broadcast_in_dim.2.azim_ref), custom_call_target="tpu_custom_call" | custom-call | tf_op jit(solution)/shard_map/table/pallas_call | solution.py:213
  23.6 0.0 copy-start
  23.6 1.2 %copy-done = bf16[640,1408]{1,0:T(8,128)(2,1)} copy-done((bf16[640,1408]{1,0:T(8,128)(2,1)}, bf16[640,1408]{1,0:T(8,128)(2,1)S(1)}, u32[]{:S(2)}) %copy-start) | copy-done | bytes 1802264
  24.9 0.0 copy-start.1
  24.9 1.2 %copy-done.1 = bf16[640,1280]{1,0:T(8,128)(2,1)} copy-done((bf16[640,1280]{1,0:T(8,128)(2,1)}, bf16[640,1280]{1,0:T(8,128)(2,1)S(1)}, u32[]{:S(2)}) %copy-start.1) | copy-done | bytes 1638424
  26.0 30.4 %all-to-all-done = bf16[16,5,80,128]{3,2,1,0:T(8,128)(2,1)S(1)} async-done(((bf16[16,5,80,128]{3,2,1,0:T(8,128)(2,1)}), bf16[16,5,80,128]{3,2,1,0:T(8,128)(2,1)S(1)}, u32[]{:S(2)}, u32[]{:S(2)}) %all-to-all-start) | async-done | bytes 1638432 | tf_op jit(solution)/shard_map/all_to_all | solution.py:333
  56.4 6.2 %grid_product.1 = bf16[8,10,8,2560]{3,2,1,0:T(8,128)(2,1)} custom-call(bf16[16,5,5,16,128]{4,3,2,1,0:T(8,128)(2,1)S(1)} %bitcast.3, bf16[640,1408]{1,0:T(8,128)(2,1)} %copy-done, bf16[640,1280]{1,0:T(8,128)(2,1)} %copy-done.1), custom_call_target="tpu_custom_call" | custom-call | tf_op jit(solution)/shard_map/grid_product/pallas_call | solution.py:306
Async XLA Ops:
  12.2 6.7 %copy-start.2 = (s32[640]{0:T(1024)S(1)}, s32[640]{0:T(1024)}, u32[]{:S(2)}) copy-start(s32[640]{0:T(1024)} %azim_ref.1) | copy-start | bytes 7684
  12.2 44.2 %all-to-all-start = ((bf16[16,5,80,128]{3,2,1,0:T(8,128)(2,1)}), bf16[16,5,80,128]{3,2,1,0:T(8,128)(2,1)S(1)}, u32[]{:S(2)}, u32[]{:S(2)}) async-start(bf16[16,5,80,128]{3,2,1,0:T(8,128)(2,1)} %legendre.1), calls=%async_computation | async-start | bytes 3276800 | tf_op jit(solution)/shard_map/all_to_all | solution.py:333
  23.6 1.2 %copy-start = (bf16[640,1408]{1,0:T(8,128)(2,1)}, bf16[640,1408]{1,0:T(8,128)(2,1)S(1)}, u32[]{:S(2)}) copy-start(bf16[640,1408]{1,0:T(8,128)(2,1)S(1)} %get-tuple-element.7.cos_hbm) | copy-start | bytes 5406724
  24.9 1.2 %copy-start.1 = (bf16[640,1280]{1,0:T(8,128)(2,1)}, bf16[640,1280]{1,0:T(8,128)(2,1)S(1)}, u32[]{:S(2)}) copy-start(bf16[640,1280]{1,0:T(8,128)(2,1)S(1)} %get-tuple-element.8.sin_hbm) | copy-start | bytes 4915204

commit v5 on v4

--- a/solution.py
+++ b/solution.py
@@ -10,6 +10,9 @@
 LANES = 128
 SUBLANES = 8
 GROUP = 2
+EARLY = 2
+NEAR = 4
+
 full_circle_radians = 6.283185307179586
 
 
@@ -63,10 +66,11 @@
 
 
 def legendre_kernel(
-    azim_ref, arr_ref, fwd_ref, back_ref, cel_ref, therm_ref, rhs_ref, polar_ref, out_ref,
-    nat_ref, pad_ref, *, levels, slots, nlat, waves
+    azim_ref, arr_ref, fwd_ref, back_ref, cel_ref, therm_ref, rhs_ref, polar_ref, *refs,
+    levels, slots, nlat, waves, begin, near
 ):
     tiles = waves // LANES
+    out_refs, (nat_ref, pad_ref) = refs[:-2], refs[-2:]
     rows = rhs_ref.shape[0]
     pitch = row_pitch()
     apart = slot_pitch(nlat)
@@ -75,7 +79,8 @@
     def rhs(row, t):
         return rhs_ref[row, :, t * LANES : (t + 1) * LANES]
 
-    first = lax.axis_index("lat") * slots + step * SUBLANES
+    mine = lax.axis_index("lat")
+    first = mine * slots + (begin + step) * SUBLANES
     sub = lax.broadcasted_iota(jnp.int32, (SUBLANES, LANES), 0)
     lane = lax.broadcasted_iota(jnp.int32, (SUBLANES, LANES), 1)
     label = jnp.zeros((SUBLANES, LANES), jnp.int32)
@@ -136,13 +141,16 @@
 
     half = LANES // 2
     low = lane < half
-    pairs = out_ref.shape[1] // (2 * SUBLANES)
+    pairs = out_refs[0].shape[1] // (2 * SUBLANES)
     for p in range(nlat // 2):
-        a = nat_ref[pl.ds(arr_ref[2 * p], SUBLANES, stride=apart), :]
-        b = nat_ref[pl.ds(arr_ref[2 * p + 1], SUBLANES, stride=apart), :]
+        d, q = divmod(p, pairs)
+        at = ((mine ^ d if near else d) * pairs + q) * 2
+        a = nat_ref[pl.ds(arr_ref[at], SUBLANES, stride=apart), :]
+        b = nat_ref[pl.ds(arr_ref[at + 1], SUBLANES, stride=apart), :]
         real = jnp.where(low, a, pltpu.roll(b, half, 1))
         imag = jnp.where(low, pltpu.roll(a, half, 1), b)
-        out_ref[p // pairs, pl.ds(p % pairs * 2 * SUBLANES, 2 * SUBLANES), :] = jnp.concatenate(
+        group, place = divmod(d, out_refs[0].shape[0])
+        out_refs[group][place, pl.ds(q * 2 * SUBLANES, 2 * SUBLANES), :] = jnp.concatenate(
             [real, imag], 0
         ).astype(jnp.bfloat16)
 
@@ -155,27 +163,31 @@
     return nlat + 4
 
 
-def legendre(rhs, azimuthal, arrangement, polar, forward, back, celerity, thermal):
+def legendre(
+    rhs, azimuthal, arrangement, polar, forward, back, celerity, thermal, begin, steps, near=0
+):
     fields, levels = rhs.shape[:2]
     slots, nlat, waves = polar.shape
     rows = fields * levels * 2
     tiles = waves // LANES
     devices = lax.axis_size("lat")
-    steps = slots // SUBLANES
     depth = nlat // devices * SUBLANES
     scalars = (azimuthal, arrangement, forward, back, celerity, thermal)
+    group = near or devices
+    outs = devices // group
     return pl.pallas_call(
         functools.partial(
-            legendre_kernel, levels=levels, slots=slots, nlat=nlat, waves=waves
+            legendre_kernel,
+            levels=levels, slots=slots, nlat=nlat, waves=waves, begin=begin, near=near,
         ),
         grid=(steps,),
         in_specs=[pl.BlockSpec(memory_space=pltpu.SMEM)] * len(scalars)
         + [
-            pl.BlockSpec((rows, SUBLANES, waves), lambda i: (0, i, 0)),
-            pl.BlockSpec((SUBLANES, nlat, waves), lambda i: (i, 0, 0)),
+            pl.BlockSpec((rows, SUBLANES, waves), lambda i: (0, begin + i, 0)),
+            pl.BlockSpec((SUBLANES, nlat, waves), lambda i: (begin + i, 0, 0)),
         ],
-        out_specs=pl.BlockSpec((devices, None, depth, LANES), lambda i: (0, i, 0, 0)),
-        out_shape=jax.ShapeDtypeStruct((devices, steps, depth, LANES), jnp.bfloat16),
+        out_specs=[pl.BlockSpec((group, None, depth, LANES), lambda i: (0, i, 0, 0))] * outs,
+        out_shape=[jax.ShapeDtypeStruct((group, steps, depth, LANES), jnp.bfloat16)] * outs,
         scratch_shapes=[
             pltpu.VMEM((SUBLANES * slot_pitch(nlat), LANES), jnp.float32),
             pltpu.VMEM((tiles, rows * row_pitch(), LANES), jnp.float32),
@@ -185,9 +197,8 @@
     )(*scalars, rhs.reshape(rows, slots, waves), polar)
 
 
-def table_kernel(azim_ref, cos_ref, sin_ref, *, nlon):
+def table_rows(m, cos_ref, sin_ref, nlon):
     blocks = nlon // LANES
-    m = azim_ref[...]
     lane = lax.broadcasted_iota(jnp.int32, m.shape, 1)
     unit = full_circle_radians / nlon
     fine = ((m * lane) % nlon).astype(jnp.float32) * unit
@@ -206,32 +217,46 @@
             sin_ref[:, at] = (-(sin_fine * cc + cos_fine * sc)).astype(jnp.bfloat16)
 
 
-def table(azimuthal, rows):
-    count = azimuthal.shape[0]
+def table_kernel(azim_ref, *refs, nlon, early, near):
+    step = pl.program_id(0)
+    mine = lax.axis_index("lat")
+    devices = azim_ref.shape[0]
+    groups = devices // near
+    ones, others = [], []
+    for i in range(2):
+        d = 2 * step + i
+        ones.append(azim_ref[mine ^ (d % groups * near + d // groups), :early])
+        others.append(azim_ref[d, early:])
+    table_rows(jnp.concatenate(ones, 0), refs[0], refs[1], nlon)
+    table_rows(jnp.concatenate(others, 0), refs[2], refs[3], nlon)
+
+
+def tables(azimuthal, devices, early, near):
+    slots = azimuthal.shape[0] // devices
     half = NLON // 2
-    spread = jnp.broadcast_to(azimuthal[:, None], (count, LANES))
+    spread = jnp.broadcast_to(azimuthal.reshape(devices, slots, 1), (devices, slots, LANES))
+    widths = (half + LANES, half) * 2
+    counts = (early, early, slots - early, slots - early)
     return pl.pallas_call(
-        functools.partial(table_kernel, nlon=NLON),
-        grid=(count // rows,),
-        in_specs=[pl.BlockSpec((rows, LANES), lambda d: (d, 0))],
-        out_specs=[
-            pl.BlockSpec((rows, half + LANES), lambda d: (d, 0)),
-            pl.BlockSpec((rows, half), lambda d: (d, 0)),
-        ],
+        functools.partial(table_kernel, nlon=NLON, early=early, near=near),
+        grid=(devices // 2,),
+        in_specs=[pl.BlockSpec(memory_space=pltpu.VMEM)],
+        out_specs=[pl.BlockSpec((2 * n, w), lambda d: (d, 0)) for n, w in zip(counts, widths)],
         out_shape=[
-            jax.ShapeDtypeStruct((count, half + LANES), jnp.bfloat16),
-            jax.ShapeDtypeStruct((count, half), jnp.bfloat16),
+            jax.ShapeDtypeStruct((devices * n, w), jnp.bfloat16) for n, w in zip(counts, widths)
         ],
         compiler_params=pltpu.CompilerParams(vmem_limit_bytes=16 * 1024 * 1024),
-        name="table",
+        name="tables",
     )(spread)
 
 
 def grid_kernel(
-    x_ref, cos_hbm, sin_hbm, out_hbm, cos_ref, sin_ref, real_ref, imag_ref, out_ref,
-    cos_sem, sin_sem, out_sem, *, fields, lat_dev, block,
+    *refs, near, fields, lat_dev, block
 ):
-    depth, width = sin_ref.shape
+    early_refs, late_ref, tables, out_hbm = refs[:near], refs[near], refs[near + 1 : near + 5], refs[near + 5]
+    cos_ref, sin_ref, real_ref, imag_ref, out_ref, load_sem, out_sem = refs[near + 6 :]
+    width = sin_ref.shape[1]
+    early = tables[0].shape[0]
     nlon = 2 * width
     half = LANES // 2
     levels = half // fields
@@ -240,29 +265,38 @@
     def span(i):
         return pl.ds(i * block, block)
 
+    def load(i, columns, which):
+        copies = []
+        for n in which:
+            ref = (cos_ref, sin_ref)[n % 2]
+            rows = pl.ds(n // 2 * early, tables[n].shape[0])
+            copies.append(
+                pltpu.make_async_copy(
+                    tables[n].at[:, columns], ref.at[rows, columns], load_sem.at[i, n]
+                )
+            )
+            copies[-1].start()
+        return copies
+
     tail = pl.ds(width, LANES)
-    ends = pltpu.make_async_copy(
-        cos_hbm.at[:, tail], cos_ref.at[:, tail], cos_sem.at[len(order)]
-    )
-    loads = {}
-    ends.start()
-    for i in order:
-        loads[i] = [
-            pltpu.make_async_copy(cos_hbm.at[:, span(i)], cos_ref.at[:, span(i)], cos_sem.at[i]),
-            pltpu.make_async_copy(sin_hbm.at[:, span(i)], sin_ref.at[:, span(i)], sin_sem.at[i]),
-        ]
-        for copy in loads[i]:
-            copy.start()
+    ends = load(len(order), tail, (0, 2))
+    loads = {i: load(i, span(i), range(4)) for i in order}
 
     for p in range(lat_dev // 2):
-        rows = x_ref[:, :, p].astype(jnp.float32)
-        for c, ref in enumerate((real_ref, imag_ref)):
-            part = rows[:, :, c * SUBLANES : (c + 1) * SUBLANES].reshape(depth, LANES)
-            ref[pl.ds(p * LANES, LANES), :] = part.astype(jnp.bfloat16).T
+        first = jnp.concatenate([ref[:, :, p] for ref in early_refs], 0).astype(jnp.float32)
+        later = late_ref[:, :, p].astype(jnp.float32)
+        at = 0
+        for rows in (first, later):
+            count = rows.shape[0] * rows.shape[1] * SUBLANES
+            for c, ref in enumerate((real_ref, imag_ref)):
+                part = rows[:, :, c * SUBLANES : (c + 1) * SUBLANES].reshape(count, LANES)
+                ref[pl.ds(p * LANES, LANES), pl.ds(at, count)] = part.astype(jnp.bfloat16).T
+            at += count
 
     lane = lax.broadcasted_iota(jnp.int32, (lat_dev * half, LANES), 1)
     mirror = (LANES - lane) % LANES
-    ends.wait()
+    for copy in ends:
+        copy.wait()
     after = jnp.dot(real_ref[...], cos_ref[:, tail], preferred_element_type=jnp.float32)
     stores = []
     for n, i in enumerate(order):
@@ -295,44 +329,60 @@
         copy.wait()
 
 
-def grid_product(received, cos, sin, lat_dev, fields, block=256):
-    devices, steps = received.shape[:2]
-    depth, width = sin.shape
+def grid_product(early, late, tabs, lat_dev, fields, block=256):
+    near = len(early)
+    width = tabs[1].shape[1]
+    depth = tabs[1].shape[0] + tabs[3].shape[0]
     half = LANES // 2
     levels = half // fields
     count = width // block
-    x = received.reshape(devices, steps, lat_dev // 2, 2 * SUBLANES, LANES)
+    parts = [
+        x.reshape(*x.shape[:2], lat_dev // 2, 2 * SUBLANES, LANES) for x in (*early, late)
+    ]
     hbm = pl.BlockSpec(memory_space=pltpu.HBM)
     out = pl.pallas_call(
-        functools.partial(grid_kernel, fields=fields, lat_dev=lat_dev, block=block),
-        in_specs=[pl.BlockSpec(memory_space=pltpu.VMEM), hbm, hbm],
+        functools.partial(grid_kernel, near=near, fields=fields, lat_dev=lat_dev, block=block),
+        in_specs=[pl.BlockSpec(memory_space=pltpu.VMEM)] * len(parts) + [hbm] * len(tabs),
         out_specs=hbm,
         out_shape=jax.ShapeDtypeStruct((fields, lat_dev, levels, 2 * width), jnp.bfloat16),
         scratch_shapes=[
-            pltpu.VMEM(cos.shape, jnp.bfloat16),
-            pltpu.VMEM(sin.shape, jnp.bfloat16),
+            pltpu.VMEM((depth, width + LANES), jnp.bfloat16),
+            pltpu.VMEM((depth, width), jnp.bfloat16),
             pltpu.VMEM((lat_dev * half, depth), jnp.bfloat16),
             pltpu.VMEM((lat_dev * half, depth), jnp.bfloat16),
             pltpu.VMEM((count, 2, fields, lat_dev, levels, block), jnp.bfloat16),
-            pltpu.SemaphoreType.DMA((count + 1,)),
-            pltpu.SemaphoreType.DMA((count,)),
+            pltpu.SemaphoreType.DMA((count + 1, len(tabs))),
             pltpu.SemaphoreType.DMA((count, 2)),
         ],
         compiler_params=pltpu.CompilerParams(vmem_limit_bytes=40 * 1024 * 1024),
         name="grid_product",
-    )(x, *(pltpu.with_memory_space_constraint(a, pltpu.HBM) for a in (cos, sin)))
+    )(*parts, *(pltpu.with_memory_space_constraint(a, pltpu.HBM) for a in tabs))
     return jnp.swapaxes(out, 1, 2)
 
 
 def per_device(rhs, azimuthal, arrangement, polar, forward, back, celerity, thermal):
-    fields, levels = rhs.shape[:2]
-    slots, nlat, waves = polar.shape
+    fields = rhs.shape[0]
+    slots, nlat, _ = polar.shape
     devices = lax.axis_size("lat")
     lat_dev = nlat // devices
-    packed = legendre(rhs, azimuthal, arrangement, polar, forward, back, celerity, thermal)
-    received = lax.all_to_all(packed, "lat", split_axis=0, concat_axis=0, tiled=True)
-    cos, sin = table(azimuthal, 2 * slots)
-    return grid_product(received, cos, sin, lat_dev, fields)
+    steps = slots // SUBLANES
+    operands = (rhs, azimuthal, arrangement, polar, forward, back, celerity, thermal)
+
+    def swap(x, distance):
+        return lax.ppermute(x, "lat", [(d, d ^ distance) for d in range(devices)])
+
+    mine = legendre(*operands, 0, EARLY, NEAR)
+    got = [mine[0]]
+    for g in range(1, devices // NEAR):
+        got.append(swap(mine[g], g * NEAR))
+    (packed,) = legendre(*operands, EARLY, steps - EARLY)
+    late = lax.all_to_all(packed, "lat", split_axis=0, concat_axis=0, tiled=True)
+    early = []
+    for j in range(NEAR):
+        part = jnp.concatenate([x[j : j + 1] for x in got], 0)
+        early.append(swap(part, j) if j else part)
+    tabs = tables(azimuthal, devices, EARLY * SUBLANES, NEAR)
+    return grid_product(early, late, tabs, lat_dev, fields)
 
 
 def solution(mesh):
@@ -357,6 +407,9 @@
             and lat_dev % 2 == 0
             and 2 * rhs.shape[0] * rhs.shape[1] == LANES
             and rhs.shape[0] > 2
+            and slots // SUBLANES > EARLY
+            and lax.axis_size("lat") % NEAR == 0
+            and lax.axis_size("lat") & (lax.axis_size("lat") - 1) == 0
         )
         form = per_device if fits else per_device_plain
         return form(rhs, azimuthal, arrangement, polar, *matrices)

time: 62.9 us -> 70.7 us (1.12)
  starting transfers between devices: 6.65 us -> 12 us
  waiting for transfers between devices: 30.4 us -> 27.5 us
  Pallas kernels: 23.1 us -> 25.8 us
  local copies, waits for them, and re-layouts: 2.54 us -> 4.77 us
    all_to_all x1, waiting for transfers between devices: 30.4 us -> 0.01 us  [per_device(): lax.all_to_all(packed, 'lat', split_axis=0, concat_axis=0, tiled=True)]
    ppermute x0 -> x6, waiting for transfers between devices: none -> 27.5 us  [swap(): return lax.ppermute(x, 'lat', [(d, d ^ distance) for d in range(devices)])]
    ppermute x0 -> x6, starting transfers between devices: none -> 5.52 us  [swap(): return lax.ppermute(x, 'lat', [(d, d ^ distance) for d in range(devices)])]
    pallas_call x1 -> x2, Pallas kernels: 12.2 us -> 14.4 us  [legendre(): pl.pallas_call(functools.partial(legendre_kernel, levels=levels, slots=sl...]
    unnamed x6 -> x10, local copies, waits for them, and re-layouts: 2.41 us -> 3.67 us
    slice x0 -> x4, local copies, waits for them, and re-layouts: none -> 0.88 us  [per_device(): part = jnp.concatenate([x[j:j + 1] for x in got], 0)]
  transfers between devices with their start and end apart: 1 -> 7, of which waited for: 1 -> 3; matrix products, arithmetic and copies ran while one was open for 0% -> 2% of each run, Pallas kernels for 7% -> 15%
where the time goes in v5:
time: 70.7 us; the launch traced here: 70.4 us
  waiting for transfers between devices  27.5 us (39%)
  Pallas kernels  25.8 us (36%)
  starting transfers between devices  12 us (17%)
  local copies, waits for them, and re-layouts  4.77 us (7%)
    ppermute x6, waiting for transfers between devices, swap(): return lax.ppermute(x, 'lat', [(d, d ^ distance) for d in range(devices)])  27.5 us
    pallas_call x2, Pallas kernels, legendre(): pl.pallas_call(functools.partial(legendre_kernel, levels=levels, slots=sl...  14.4 us
    pallas_call x1, Pallas kernels, grid_product(): pl.pallas_call(functools.partial(grid_kernel, near=near, fields=fields, l...  6.72 us
    all_to_all x1, starting transfers between devices, per_device(): lax.all_to_all(packed, 'lat', split_axis=0, concat_axis=0, tiled=True)  6.52 us
    ppermute x6, starting transfers between devices, swap(): return lax.ppermute(x, 'lat', [(d, d ^ distance) for d in range(devices)])  5.52 us
    pallas_call x1, Pallas kernels, tables(): pl.pallas_call(functools.partial(table_kernel, nlon=NLON, early=early, ne...  4.68 us
    unnamed x10, local copies, waits for them, and re-layouts  3.67 us
  transfers between devices with their start and end apart: 7, of which 3 were waited for; matrix products, arithmetic and copies ran while one was open for 2% of the time, Pallas kernels for 15%

profile of v5, /device:TPU:13, one launch (start us, length us, event | category | flops | bytes accessed | tf_op | source)
XLA Modules:
  0.0 70.4 jit_solution(11943575425584422645)
XLA Ops:
  0.0 8.3 %legendre.3 = bf16[16,3,80,128]{3,2,1,0:T(8,128)(2,1)} custom-call(s32[640]{0:T(1024)} %azim_ref.3, s32[160]{0:T(256)} %arr_ref.3, f32[8,8]{1,0:T(8,128)} %fwd_ref.3, f32[8,8]{1,0:T(8,128)} %back_ref.3, f32[8]{0:T(128)} %cel_ref.3, f32[8,8]{1,0:T(8,128)} %therm_ref.3, f32[128,40,640]{2,1,0:T(8,128)} %bitcast.12, bf16[40,160,640]{2,1,0:T(8,128)(2,1)} %polar_ref.3), custom_call_target="tpu_custom_call" | custom-call | tf_op jit(solution)/shard_map/legendre/pallas_call | solution.py:178
  8.3 6.5 %all-to-all-start = ((bf16[16,3,80,128]{3,2,1,0:T(8,128)(2,1)}), bf16[16,3,80,128]{3,2,1,0:T(8,128)(2,1)S(1)}, u32[]{:S(2)}, u32[]{:S(2)}) async-start(bf16[16,3,80,128]{3,2,1,0:T(8,128)(2,1)} %legendre.3), calls=%async_computation | async-start | bytes 1966080 | tf_op jit(solution)/shard_map/all_to_all | solution.py:379
  14.8 6.1 %legendre.2 = (bf16[4,2,80,128]{3,2,1,0:T(8,128)(2,1)}, bf16[4,2,80,128]{3,2,1,0:T(8,128)(2,1)}, bf16[4,2,80,128]{3,2,1,0:T(8,128)(2,1)}, bf16[4,2,80,128]{3,2,1,0:T(8,128)(2,1)}) custom-call(s32[640]{0:T(1024)} %azim_ref.3, s32[160]{0:T(256)} %arr_ref.3, f32[8,8]{1,0:T(8,128)} %fwd_ref.3, f32[8,8]{1,0:T(8,128)} %back_ref.3, f32[8]{0:T(128)} %cel_ref.3, ...), custom_call_target="tpu_custom_call" | custom-call | tf_op jit(solution)/shard_map/legendre/pallas_call | solution.py:178
  20.9 0.3 collective-permute-start
  21.3 2.1 %collective-permute-start.1 = (bf16[4,2,80,128]{3,2,1,0:T(8,128)(2,1)}, bf16[4,2,80,128]{3,2,1,0:T(8,128)(2,1)S(1)}, u32[]{:S(2)}, u32[]{:S(2)}) collective-permute-start(bf16[4,2,80,128]{3,2,1,0:T(8,128)(2,1)} %get-tuple-element.15), channel_id=1, source_target_pairs={{0,8},{1,9},{2,10},{3,11},{4,12},{5,13},{6,14},{7,15},{8,0},{9,1},... | collective-permute-start | bytes 491528 | tf_op jit(solution)/shard_map/ppermute | solution.py:372
  23.4 0.3 collective-permute-start.2
  23.6 0.8 %fusion = (bf16[1,2,80,128]{3,2,1,0:T(8,128)(2,1)S(1)}, bf16[1,2,80,128]{3,2,1,0:T(8,128)(2,1)S(1)}, bf16[1,2,80,128]{3,2,1,0:T(8,128)(2,1)S(1)}, bf16[1,2,80,128]{3,2,1,0:T(8,128)(2,1)S(1)}) fusion(bf16[4,2,80,128]{3,2,1,0:T(8,128)(2,1)} %get-tuple-element.13), kind=kLoop, calls=%fused_computation.4 | loop fusion | bytes 327680 | tf_op jit(solution)/shard_map/slice | solution.py:382
  24.5 10.9 %collective-permute-done = bf16[4,2,80,128]{3,2,1,0:T(8,128)(2,1)S(1)} collective-permute-done((bf16[4,2,80,128]{3,2,1,0:T(8,128)(2,1)}, bf16[4,2,80,128]{3,2,1,0:T(8,128)(2,1)S(1)}, u32[]{:S(2)}, u32[]{:S(2)}) %collective-permute-start) | collective-permute-done | bytes 163872 | tf_op jit(solution)/shard_map/ppermute | solution.py:372
  35.4 11.4 %collective-permute-done.1 = bf16[4,2,80,128]{3,2,1,0:T(8,128)(2,1)S(1)} collective-permute-done((bf16[4,2,80,128]{3,2,1,0:T(8,128)(2,1)}, bf16[4,2,80,128]{3,2,1,0:T(8,128)(2,1)S(1)}, u32[]{:S(2)}, u32[]{:S(2)}) %collective-permute-start.1) | collective-permute-done | bytes 163872 | tf_op jit(solution)/shard_map/ppermute | solution.py:372
  46.8 5.3 %collective-permute-done.2 = bf16[4,2,80,128]{3,2,1,0:T(8,128)(2,1)S(1)} collective-permute-done((bf16[4,2,80,128]{3,2,1,0:T(8,128)(2,1)}, bf16[4,2,80,128]{3,2,1,0:T(8,128)(2,1)S(1)}, u32[]{:S(2)}, u32[]{:S(2)}) %collective-permute-start.2) | collective-permute-done | bytes 163872 | tf_op jit(solution)/shard_map/ppermute | solution.py:372
  52.1 1.0 %collective-permute-start.3 = (bf16[4,2,80,128]{3,2,1,0:T(8,128)(2,1)S(1)}, bf16[4,2,80,128]{3,2,1,0:T(8,128)(2,1)S(1)}, u32[]{:S(2)}, u32[]{:S(2)}) collective-permute-start(bf16[4,2,80,128]{3,2,1,0:T(8,128)(2,1)S(1)} %pad_maximum_fusion.1), channel_id=1, source_target_pairs={{0,1},{1,0},{2,3},{3,2},{4,5},{5,4},{6,7},{7,6},{8,9},{9,8},{10,11... | collective-permute-start | bytes 491528 | tf_op jit(solution)/shard_map/ppermute | solution.py:372
  53.2 0.3 collective-permute-start.4
  53.5 1.4 %collective-permute-start.5 = (bf16[4,2,80,128]{3,2,1,0:T(8,128)(2,1)S(1)}, bf16[4,2,80,128]{3,2,1,0:T(8,128)(2,1)S(1)}, u32[]{:S(2)}, u32[]{:S(2)}) collective-permute-start(bf16[4,2,80,128]{3,2,1,0:T(8,128)(2,1)S(1)} %pad_maximum_fusion.3), channel_id=1, source_target_pairs={{0,3},{1,2},{2,1},{3,0},{4,7},{5,6},{6,5},{7,4},{8,11},{9,10},{10,... | collective-permute-start | bytes 491528 | tf_op jit(solution)/shard_map/ppermute | solution.py:372
  55.0 0.1 broadcast_in_dim.7
  55.1 0.1 broadcast_in_dim.8.azim_ref
  55.2 4.7 %tables.1 = (bf16[256,1408]{1,0:T(8,128)(2,1)S(1)}, bf16[256,1280]{1,0:T(8,128)(2,1)S(1)}, bf16[384,1408]{1,0:T(8,128)(2,1)S(1)}, bf16[384,1280]{1,0:T(8,128)(2,1)S(1)}) custom-call(s32[16,40,128]{2,1,0:T(8,128)S(1)} %broadcast_in_dim.8.azim_ref), custom_call_target="tpu_custom_call" | custom-call | tf_op jit(solution)/shard_map/tables/pallas_call | solution.py:240
  59.9 1.0 %copy-done = bf16[384,1408]{1,0:T(8,128)(2,1)} copy-done((bf16[384,1408]{1,0:T(8,128)(2,1)}, bf16[384,1408]{1,0:T(8,128)(2,1)S(1)}, u32[]{:S(2)}) %copy-start) | copy-done | bytes 1081368
  60.9 1.0 %copy-done.1 = bf16[384,1280]{1,0:T(8,128)(2,1)} copy-done((bf16[384,1280]{1,0:T(8,128)(2,1)}, bf16[384,1280]{1,0:T(8,128)(2,1)S(1)}, u32[]{:S(2)}) %copy-start.1) | copy-done | bytes 983064
  61.9 0.9 %copy-done.2 = bf16[256,1408]{1,0:T(8,128)(2,1)} copy-done((bf16[256,1408]{1,0:T(8,128)(2,1)}, bf16[256,1408]{1,0:T(8,128)(2,1)S(1)}, u32[]{:S(2)}) %copy-start.2) | copy-done | bytes 720920
  62.7 0.8 %copy-done.3 = bf16[256,1280]{1,0:T(8,128)(2,1)} copy-done((bf16[256,1280]{1,0:T(8,128)(2,1)}, bf16[256,1280]{1,0:T(8,128)(2,1)S(1)}, u32[]{:S(2)}) %copy-start.3) | copy-done | bytes 655384
  63.6 0.0 collective-permute-done.3
  63.6 0.0 collective-permute-done.4
  63.6 0.0 all-to-all-done
  63.6 6.7 %grid_product.1 = bf16[8,10,8,2560]{3,2,1,0:T(8,128)(2,1)} custom-call(bf16[4,2,5,16,128]{4,3,2,1,0:T(8,128)(2,1)S(1)} %bitcast.8, bf16[4,2,5,16,128]{4,3,2,1,0:T(8,128)(2,1)S(1)} %bitcast.9, bf16[4,2,5,16,128]{4,3,2,1,0:T(8,128)(2,1)S(1)} %bitcast.10, bf16[4,2,5,16,128]{4,3,2,1,0:T(8,128)(2,1)S(1)} %bitcast.11, bf16[16,3,5,16,128]{4,3,2,1,0:T(8,128)(2,1)S(1)} %bitcast.7, ...), custom_call_target="tpu_custom_call" | custom-call | tf_op jit(solution)/shard_map/grid_product/pallas_call | solution.py:343
  (14 shorter events, 0.1 us)
Async XLA Ops:
  8.3 55.3 %all-to-all-start = ((bf16[16,3,80,128]{3,2,1,0:T(8,128)(2,1)}), bf16[16,3,80,128]{3,2,1,0:T(8,128)(2,1)S(1)}, u32[]{:S(2)}, u32[]{:S(2)}) async-start(bf16[16,3,80,128]{3,2,1,0:T(8,128)(2,1)} %legendre.3), calls=%async_computation | async-start | bytes 1966080 | tf_op jit(solution)/shard_map/all_to_all | solution.py:379
  14.8 40.1 %copy-start.4 = (s32[640]{0:T(1024)S(1)}, s32[640]{0:T(1024)}, u32[]{:S(2)}) copy-start(s32[640]{0:T(1024)} %azim_ref.3) | copy-start | bytes 7684
  20.9 14.4 %collective-permute-start = (bf16[4,2,80,128]{3,2,1,0:T(8,128)(2,1)}, bf16[4,2,80,128]{3,2,1,0:T(8,128)(2,1)S(1)}, u32[]{:S(2)}, u32[]{:S(2)}) collective-permute-start(bf16[4,2,80,128]{3,2,1,0:T(8,128)(2,1)} %get-tuple-element.14), channel_id=1, source_target_pairs={{0,4},{1,5},{2,6},{3,7},{4,0},{5,1},{6,2},{7,3},{8,12},{9,13},{10,... | collective-permute-start | bytes 491528 | tf_op jit(solution)/shard_map/ppermute | solution.py:372
  21.3 25.5 %collective-permute-start.1 = (bf16[4,2,80,128]{3,2,1,0:T(8,128)(2,1)}, bf16[4,2,80,128]{3,2,1,0:T(8,128)(2,1)S(1)}, u32[]{:S(2)}, u32[]{:S(2)}) collective-permute-start(bf16[4,2,80,128]{3,2,1,0:T(8,128)(2,1)} %get-tuple-element.15), channel_id=1, source_target_pairs={{0,8},{1,9},{2,10},{3,11},{4,12},{5,13},{6,14},{7,15},{8,0},{9,1},... | collective-permute-start | bytes 491528 | tf_op jit(solution)/shard_map/ppermute | solution.py:372
  23.4 28.7 %collective-permute-start.2 = (bf16[4,2,80,128]{3,2,1,0:T(8,128)(2,1)}, bf16[4,2,80,128]{3,2,1,0:T(8,128)(2,1)S(1)}, u32[]{:S(2)}, u32[]{:S(2)}) collective-permute-start(bf16[4,2,80,128]{3,2,1,0:T(8,128)(2,1)} %get-tuple-element.16), channel_id=1, source_target_pairs={{0,12},{1,13},{2,14},{3,15},{4,8},{5,9},{6,10},{7,11},{8,4},{9,5},... | collective-permute-start | bytes 491528 | tf_op jit(solution)/shard_map/ppermute | solution.py:372
  52.1 11.5 %collective-permute-start.3 = (bf16[4,2,80,128]{3,2,1,0:T(8,128)(2,1)S(1)}, bf16[4,2,80,128]{3,2,1,0:T(8,128)(2,1)S(1)}, u32[]{:S(2)}, u32[]{:S(2)}) collective-permute-start(bf16[4,2,80,128]{3,2,1,0:T(8,128)(2,1)S(1)} %pad_maximum_fusion.1), channel_id=1, source_target_pairs={{0,1},{1,0},{2,3},{3,2},{4,5},{5,4},{6,7},{7,6},{8,9},{9,8},{10,11... | collective-permute-start | bytes 491528 | tf_op jit(solution)/shard_map/ppermute | solution.py:372
  53.2 10.4 %collective-permute-start.4 = (bf16[4,2,80,128]{3,2,1,0:T(8,128)(2,1)S(1)}, bf16[4,2,80,128]{3,2,1,0:T(8,128)(2,1)S(1)}, u32[]{:S(2)}, u32[]{:S(2)}) collective-permute-start(bf16[4,2,80,128]{3,2,1,0:T(8,128)(2,1)S(1)} %pad_maximum_fusion.2), channel_id=1, source_target_pairs={{0,2},{1,3},{2,0},{3,1},{4,6},{5,7},{6,4},{7,5},{8,10},{9,11},{10,... | collective-permute-start | bytes 491528 | tf_op jit(solution)/shard_map/ppermute | solution.py:372
  53.5 10.1 %collective-permute-start.5 = (bf16[4,2,80,128]{3,2,1,0:T(8,128)(2,1)S(1)}, bf16[4,2,80,128]{3,2,1,0:T(8,128)(2,1)S(1)}, u32[]{:S(2)}, u32[]{:S(2)}) collective-permute-start(bf16[4,2,80,128]{3,2,1,0:T(8,128)(2,1)S(1)} %pad_maximum_fusion.3), channel_id=1, source_target_pairs={{0,3},{1,2},{2,1},{3,0},{4,7},{5,6},{6,5},{7,4},{8,11},{9,10},{10,... | collective-permute-start | bytes 491528 | tf_op jit(solution)/shard_map/ppermute | solution.py:372
  59.9 1.0 %copy-start = (bf16[384,1408]{1,0:T(8,128)(2,1)}, bf16[384,1408]{1,0:T(8,128)(2,1)S(1)}, u32[]{:S(2)}) copy-start(bf16[384,1408]{1,0:T(8,128)(2,1)S(1)} %get-tuple-element.19.refs_7_) | copy-start | bytes 3244036
  60.9 1.0 %copy-start.1 = (bf16[384,1280]{1,0:T(8,128)(2,1)}, bf16[384,1280]{1,0:T(8,128)(2,1)S(1)}, u32[]{:S(2)}) copy-start(bf16[384,1280]{1,0:T(8,128)(2,1)S(1)} %get-tuple-element.20.refs_8_) | copy-start | bytes 2949124
  61.9 0.9 %copy-start.2 = (bf16[256,1408]{1,0:T(8,128)(2,1)}, bf16[256,1408]{1,0:T(8,128)(2,1)S(1)}, u32[]{:S(2)}) copy-start(bf16[256,1408]{1,0:T(8,128)(2,1)S(1)} %get-tuple-element.17.refs_5_) | copy-start | bytes 2162692
  62.7 0.8 %copy-start.3 = (bf16[256,1280]{1,0:T(8,128)(2,1)}, bf16[256,1280]{1,0:T(8,128)(2,1)S(1)}, u32[]{:S(2)}) copy-start(bf16[256,1280]{1,0:T(8,128)(2,1)S(1)} %get-tuple-element.18.refs_6_) | copy-start | bytes 1966084

commit v6 on v5

--- a/solution.py
+++ b/solution.py
@@ -10,6 +10,7 @@
 LANES = 128
 SUBLANES = 8
 GROUP = 2
+VMEM_MIB = 40
 EARLY = 2
 NEAR = 4
 
@@ -66,21 +67,109 @@
 
 
 def legendre_kernel(
-    azim_ref, arr_ref, fwd_ref, back_ref, cel_ref, therm_ref, rhs_ref, polar_ref, *refs,
-    levels, slots, nlat, waves, begin, near
+    *refs, levels, begin, steps, near, outs, carried, carry
 ):
+    refs = list(refs)
+    sources = [refs.pop(0) for _ in range(6)]
+    rhs_hbm, polar_hbm = refs.pop(0), refs.pop(0)
+    given = [refs.pop(0) for _ in range(2 * carried)]
+    out_hbms = [refs.pop(0) for _ in range(outs)]
+    taken = [refs.pop(0) for _ in range(2 * carry)]
+    scalars = [refs.pop(0) for _ in range(6)]
+    rhs_buf, polar_buf, nat_one, nat_two, pad_one, pad_two, stage_ref = refs[:7]
+    scalar_sem, load_sem, out_sem = refs[7:]
+    azim_ref, arr_ref, *matrices = scalars
+
+    small = [
+        pltpu.make_async_copy(src, dst, scalar_sem.at[i])
+        for i, (src, dst) in enumerate(zip(sources, scalars))
+    ]
+    for copy in small:
+        copy.start()
+
+    def load(step, targets):
+        at = pl.ds((begin + step) * SUBLANES, SUBLANES)
+        copies = [
+            pltpu.make_async_copy(rhs_hbm.at[:, at, :], targets[0], load_sem.at[step, 0]),
+            pltpu.make_async_copy(polar_hbm.at[at], targets[1], load_sem.at[step, 1]),
+        ]
+        for copy in copies:
+            copy.start()
+        return copies
+
+    blocks, loads, stores = {}, {}, []
+    for step in range(steps):
+        own = step - carried
+        blocks[step] = (rhs_buf.at[own], polar_buf.at[own]) if own >= 0 else tuple(given)
+    if carry:
+        blocks[steps] = tuple(taken)
+    for step in range(carried, min(carried + 2, steps)):
+        loads[step] = load(step, blocks[step])
+
+    def arrive(step):
+        for copy in loads.get(step, ()):
+            copy.wait()
+        after = step + 2
+        if after in blocks and after not in loads:
+            loads[after] = load(after, blocks[after])
+
+    def prepare(step):
+        pad = (pad_one, pad_two)[step % 2]
+        yield from update_parts(azim_ref, matrices, blocks[step][0], pad, begin + step, levels)
+
+    def finish(step):
+        pad, nat = ((pad_one, nat_one), (pad_two, nat_two))[step % 2]
+        outputs = [stage_ref.at[step, g] for g in range(outs)]
+        yield from product_parts(
+            azim_ref, arr_ref, blocks[step][1], pad, nat, outputs, begin + step, near
+        )
+        for g in range(outs):
+            stores.append(
+                pltpu.make_async_copy(
+                    stage_ref.at[step, g], out_hbms[g].at[:, step], out_sem.at[step, g]
+                )
+            )
+            stores[-1].start()
+
+    arrive(0)
+    for copy in small:
+        copy.wait()
+    for _ in prepare(0):
+        pass
+    for step in range(steps):
+        following = iter(())
+        if step + 1 < steps and carried:
+            arrive(step + 1)
+            following = prepare(step + 1)
+        for _ in finish(step):
+            next(following, None)
+        for _ in following:
+            pass
+        if step + 1 < steps and not carried:
+            arrive(step + 1)
+            for _ in prepare(step + 1):
+                pass
+    for copy in loads.get(steps, ()):
+        copy.wait()
+    for copy in stores:
+        copy.wait()
+
+
+def first_slot(azim_ref, step):
+    own = azim_ref.shape[0] // lax.axis_size("lat")
+    return lax.axis_index("lat") * own + step * SUBLANES
+
+
+def update_parts(azim_ref, matrices, rhs_ref, pad_ref, step, levels):
+    fwd_ref, back_ref, cel_ref, therm_ref = matrices
+    rows, _, waves = rhs_ref.shape
     tiles = waves // LANES
-    out_refs, (nat_ref, pad_ref) = refs[:-2], refs[-2:]
-    rows = rhs_ref.shape[0]
     pitch = row_pitch()
-    apart = slot_pitch(nlat)
-    step = pl.program_id(0)
+    first = first_slot(azim_ref, step)
 
     def rhs(row, t):
         return rhs_ref[row, :, t * LANES : (t + 1) * LANES]
 
-    mine = lax.axis_index("lat")
-    first = mine * slots + (begin + step) * SUBLANES
     sub = lax.broadcasted_iota(jnp.int32, (SUBLANES, LANES), 0)
     lane = lax.broadcasted_iota(jnp.int32, (SUBLANES, LANES), 1)
     label = jnp.zeros((SUBLANES, LANES), jnp.int32)
@@ -118,11 +207,20 @@
             for i, (t, c) in enumerate(parts):
                 row = (levels + l) * 2 + c
                 pad_ref[t, pl.ds(row * pitch, SUBLANES), :] = rhs(row, t) - response[i]
-
-    for t in range(tiles):
-        for row in range(4 * levels, rows):
-            pad_ref[t, pl.ds(row * pitch, SUBLANES), :] = rhs(row, t)
-
+        for t in ts:
+            for row in range(4 * levels, rows):
+                pad_ref[t, pl.ds(row * pitch, SUBLANES), :] = rhs(row, t)
+        yield
+
+
+def product_parts(azim_ref, arr_ref, polar_ref, pad_ref, nat_ref, out_refs, step, near):
+    _, nlat, waves = polar_ref.shape
+    tiles = waves // LANES
+    pitch = row_pitch()
+    apart = slot_pitch(nlat)
+    rows = pad_ref.shape[1] // pitch
+    mine = lax.axis_index("lat")
+    first = first_slot(azim_ref, step)
     for s in range(SUBLANES):
         room = waves - azim_ref[first + s]
         pieces = []
@@ -138,9 +236,10 @@
             polar_ref[s], coeffs, (((1,), (1,)), ((), ())), preferred_element_type=jnp.float32
         )
         nat_ref[pl.ds(s * apart, nlat), :] = product
+        yield
 
     half = LANES // 2
-    low = lane < half
+    low = lax.broadcasted_iota(jnp.int32, (SUBLANES, LANES), 1) < half
     pairs = out_refs[0].shape[1] // (2 * SUBLANES)
     for p in range(nlat // 2):
         d, q = divmod(p, pairs)
@@ -153,6 +252,7 @@
         out_refs[group][place, pl.ds(q * 2 * SUBLANES, 2 * SUBLANES), :] = jnp.concatenate(
             [real, imag], 0
         ).astype(jnp.bfloat16)
+    yield
 
 
 def row_pitch():
@@ -164,7 +264,8 @@
 
 
 def legendre(
-    rhs, azimuthal, arrangement, polar, forward, back, celerity, thermal, begin, steps, near=0
+    rhs, azimuthal, arrangement, polar, forward, back, celerity, thermal, begin, steps,
+    near=0, given=(), carry=False,
 ):
     fields, levels = rhs.shape[:2]
     slots, nlat, waves = polar.shape
@@ -175,26 +276,45 @@
     scalars = (azimuthal, arrangement, forward, back, celerity, thermal)
     group = near or devices
     outs = devices // group
+    carried = len(given) // 2
+    hbm = pl.BlockSpec(memory_space=pltpu.HBM)
+    vmem = pl.BlockSpec(memory_space=pltpu.VMEM)
+    rhs_block, polar_block = (rows, SUBLANES, waves), (SUBLANES, nlat, waves)
+    next_blocks = [
+        jax.ShapeDtypeStruct(rhs_block, rhs.dtype),
+        jax.ShapeDtypeStruct(polar_block, polar.dtype),
+    ]
+    own = steps - carried
     return pl.pallas_call(
         functools.partial(
-            legendre_kernel,
-            levels=levels, slots=slots, nlat=nlat, waves=waves, begin=begin, near=near,
+            legendre_kernel, levels=levels, begin=begin, steps=steps, near=near, outs=outs,
+            carried=carried, carry=int(carry),
         ),
-        grid=(steps,),
-        in_specs=[pl.BlockSpec(memory_space=pltpu.SMEM)] * len(scalars)
+        in_specs=[hbm] * (len(scalars) + 2) + [vmem] * len(given),
+        out_specs=[hbm] * outs + [vmem, vmem] * carry,
+        out_shape=[jax.ShapeDtypeStruct((group, steps, depth, LANES), jnp.bfloat16)] * outs
+        + next_blocks * carry,
+        scratch_shapes=[pltpu.SMEM(a.shape, a.dtype) for a in scalars]
         + [
-            pl.BlockSpec((rows, SUBLANES, waves), lambda i: (0, begin + i, 0)),
-            pl.BlockSpec((SUBLANES, nlat, waves), lambda i: (begin + i, 0, 0)),
+            pltpu.VMEM((own, *rhs_block), rhs.dtype),
+            pltpu.VMEM((own, *polar_block), polar.dtype),
+        ]
+        + [pltpu.VMEM((SUBLANES * slot_pitch(nlat), LANES), jnp.float32)] * 2
+        + [pltpu.VMEM((tiles, rows * row_pitch(), LANES), jnp.float32)] * 2
+        + [
+            pltpu.VMEM((steps, outs, group, depth, LANES), jnp.bfloat16),
+            pltpu.SemaphoreType.DMA((len(scalars),)),
+            pltpu.SemaphoreType.DMA((steps + 1, 2)),
+            pltpu.SemaphoreType.DMA((steps, outs)),
         ],
-        out_specs=[pl.BlockSpec((group, None, depth, LANES), lambda i: (0, i, 0, 0))] * outs,
-        out_shape=[jax.ShapeDtypeStruct((group, steps, depth, LANES), jnp.bfloat16)] * outs,
-        scratch_shapes=[
-            pltpu.VMEM((SUBLANES * slot_pitch(nlat), LANES), jnp.float32),
-            pltpu.VMEM((tiles, rows * row_pitch(), LANES), jnp.float32),
-        ],
-        compiler_params=pltpu.CompilerParams(vmem_limit_bytes=60 * 1024 * 1024),
+        compiler_params=pltpu.CompilerParams(vmem_limit_bytes=VMEM_MIB * 1024 * 1024),
         name="legendre",
-    )(*scalars, rhs.reshape(rows, slots, waves), polar)
+    )(
+        *(pltpu.with_memory_space_constraint(a, pltpu.HBM) for a in scalars),
+        pltpu.with_memory_space_constraint(rhs.reshape(rows, slots, waves), pltpu.HBM),
+        pltpu.with_memory_space_constraint(polar, pltpu.HBM),
+        *(pltpu.with_memory_space_constraint(a, pltpu.VMEM) for a in given),
+    )
 
 
 def table_rows(m, cos_ref, sin_ref, nlon):
@@ -371,11 +491,13 @@
     def swap(x, distance):
         return lax.ppermute(x, "lat", [(d, d ^ distance) for d in range(devices)])
 
-    mine = legendre(*operands, 0, EARLY, NEAR)
+    *mine, next_rhs, next_polar = legendre(*operands, 0, EARLY, NEAR, carry=True)
     got = [mine[0]]
     for g in range(1, devices // NEAR):
         got.append(swap(mine[g], g * NEAR))
-    (packed,) = legendre(*operands, EARLY, steps - EARLY)
+    (packed,) = legendre(
+        *operands, EARLY, steps - EARLY, given=(next_rhs, next_polar)
+    )
     late = lax.all_to_all(packed, "lat", split_axis=0, concat_axis=0, tiled=True)
     early = []
     for j in range(NEAR):

time: 70.7 us -> 74.9 us (1.059)
  waiting for transfers between devices: 27.5 us -> 34.5 us
  Pallas kernels: 25.8 us -> 23.9 us
  local copies, waits for them, and re-layouts: 4.77 us -> 3.94 us
    ppermute x6, waiting for transfers between devices: 27.5 us -> 34.5 us  [swap(): return lax.ppermute(x, 'lat', [(d, d ^ distance) for d in range(devices)])]
    pallas_call x2, Pallas kernels: 14.4 us -> 12.5 us  [legendre(): pl.pallas_call(functools.partial(legendre_kernel, levels=levels, begin=be...]
    slice x4, local copies, waits for them, and re-layouts: 0.88 us -> 0.05 us  [per_device(): part = jnp.concatenate([x[j:j + 1] for x in got], 0)]
  transfers between devices with their start and end apart: 7 -> 7, of which waited for: 3 -> 3; matrix products, arithmetic and copies ran while one was open for 2% -> 0% of each run, Pallas kernels for 15% -> 6%
where the time goes in v6:
time: 74.9 us; the launch traced here: 74.5 us
  waiting for transfers between devices  34.5 us (46%)
  Pallas kernels  23.9 us (32%)
  starting transfers between devices  11.8 us (16%)
  local copies, waits for them, and re-layouts  3.94 us (5%)
    ppermute x6, waiting for transfers between devices, swap(): return lax.ppermute(x, 'lat', [(d, d ^ distance) for d in range(devices)])  34.5 us
    pallas_call x2, Pallas kernels, legendre(): pl.pallas_call(functools.partial(legendre_kernel, levels=levels, begin=be...  12.5 us
    pallas_call x1, Pallas kernels, grid_product(): pl.pallas_call(functools.partial(grid_kernel, near=near, fields=fields, l...  6.72 us
    all_to_all x1, starting transfers between devices, per_device(): lax.all_to_all(packed, 'lat', split_axis=0, concat_axis=0, tiled=True)  6.53 us
    ppermute x6, starting transfers between devices, swap(): return lax.ppermute(x, 'lat', [(d, d ^ distance) for d in range(devices)])  5.23 us
    pallas_call x1, Pallas kernels, tables(): pl.pallas_call(functools.partial(table_kernel, nlon=NLON, early=early, ne...  4.68 us
    unnamed x10, local copies, waits for them, and re-layouts  3.67 us
  transfers between devices with their start and end apart: 7, of which 3 were waited for; matrix products, arithmetic and copies ran while one was open for 0% of the time, Pallas kernels for 6%

profile of v6, /device:TPU:13, one launch (start us, length us, event | category | flops | bytes accessed | tf_op | source)
XLA Modules:
  0.0 74.5 jit_solution(18078508562245289526)
XLA Ops:
  0.0 5.9 %legendre.2 = (bf16[4,2,80,128]{3,2,1,0:T(8,128)(2,1)S(1)}, bf16[4,2,80,128]{3,2,1,0:T(8,128)(2,1)S(1)}, bf16[4,2,80,128]{3,2,1,0:T(8,128)(2,1)S(1)}, bf16[4,2,8...) custom-call(s32[640]{0:T(1024)} %refs_0_.3, s32[160]{0:T(256)} %refs_1_.3, ...), custom_call_target="tpu_custom_call" | custom-call | tf_op jit(solution)/shard_map/legendre/pallas_call | solution.py:288
  5.9 6.7 %legendre.3 = bf16[16,3,80,128]{3,2,1,0:T(8,128)(2,1)} custom-call(s32[640]{0:T(1024)} %refs_0_.3, s32[160]{0:T(256)} %refs_1_.3, f32[8,8]{1,0:T(8,128)} %refs_2_.3, f32[8,8]{1,0:T(8,128)} %refs_3_.3, f32[8]{0:T(128)} %refs_4_.3, f32[8,8]{1,0:T(8,128)} %refs_5_.3, f32[128,40,640]{2,1,0:T(8,128)} %bitcast.13, bf16[40,160,640]{2,1,0:T(8,128)(2,1)} %refs_7_.3, ...), custom_call_target="tpu_custom_call" | custom-call | tf_op jit(solution)/shard_map/legendre/pallas_call | solution.py:288
  12.6 0.0 copy-start.4
  12.6 6.5 %all-to-all-start = ((bf16[16,3,80,128]{3,2,1,0:T(8,128)(2,1)}), bf16[16,3,80,128]{3,2,1,0:T(8,128)(2,1)S(1)}, u32[]{:S(2)}, u32[]{:S(2)}) async-start(bf16[16,3,80,128]{3,2,1,0:T(8,128)(2,1)} %legendre.3), calls=%async_computation | async-start | bytes 1966080 | tf_op jit(solution)/shard_map/all_to_all | solution.py:501
  19.1 0.3 collective-permute-start
  19.4 2.1 %collective-permute-start.1 = (bf16[4,2,80,128]{3,2,1,0:T(8,128)(2,1)S(1)}, bf16[4,2,80,128]{3,2,1,0:T(8,128)(2,1)S(1)}, u32[]{:S(2)}, u32[]{:S(2)}) collective-permute-start(bf16[4,2,80,128]{3,2,1,0:T(8,128)(2,1)S(1)} %get-tuple-element.17), channel_id=1, source_target_pairs={{0,8},{1,9},{2,10},{3,11},{4,12},{5,13},{6,14},{7,15},{8,0},{9,1},... | collective-permute-start | bytes 491528 | tf_op jit(solution)/shard_map/ppermute | solution.py:492
  21.5 0.3 collective-permute-start.2
  21.8 17.8 %collective-permute-done = bf16[4,2,80,128]{3,2,1,0:T(8,128)(2,1)S(1)} collective-permute-done((bf16[4,2,80,128]{3,2,1,0:T(8,128)(2,1)S(1)}, bf16[4,2,80,128]{3,2,1,0:T(8,128)(2,1)S(1)}, u32[]{:S(2)}, u32[]{:S(2)}) %collective-permute-start) | collective-permute-done | bytes 163872 | tf_op jit(solution)/shard_map/ppermute | solution.py:492
  39.7 11.3 %collective-permute-done.1 = bf16[4,2,80,128]{3,2,1,0:T(8,128)(2,1)S(1)} collective-permute-done((bf16[4,2,80,128]{3,2,1,0:T(8,128)(2,1)S(1)}, bf16[4,2,80,128]{3,2,1,0:T(8,128)(2,1)S(1)}, u32[]{:S(2)}, u32[]{:S(2)}) %collective-permute-start.1) | collective-permute-done | bytes 163872 | tf_op jit(solution)/shard_map/ppermute | solution.py:492
  50.9 5.4 %collective-permute-done.2 = bf16[4,2,80,128]{3,2,1,0:T(8,128)(2,1)S(1)} collective-permute-done((bf16[4,2,80,128]{3,2,1,0:T(8,128)(2,1)S(1)}, bf16[4,2,80,128]{3,2,1,0:T(8,128)(2,1)S(1)}, u32[]{:S(2)}, u32[]{:S(2)}) %collective-permute-start.2) | collective-permute-done | bytes 163872 | tf_op jit(solution)/shard_map/ppermute | solution.py:492
  56.4 1.2 %collective-permute-start.5 = (bf16[4,2,80,128]{3,2,1,0:T(8,128)(2,1)S(1)}, bf16[4,2,80,128]{3,2,1,0:T(8,128)(2,1)S(1)}, u32[]{:S(2)}, u32[]{:S(2)}) collective-permute-start(bf16[4,2,80,128]{3,2,1,0:T(8,128)(2,1)S(1)} %pad_maximum_fusion.3), channel_id=1, source_target_pairs={{0,3},{1,2},{2,1},{3,0},{4,7},{5,6},{6,5},{7,4},{8,11},{9,10},{10,... | collective-permute-start | bytes 491528 | tf_op jit(solution)/shard_map/ppermute | solution.py:492
  57.6 1.2 %collective-permute-start.4 = (bf16[4,2,80,128]{3,2,1,0:T(8,128)(2,1)S(1)}, bf16[4,2,80,128]{3,2,1,0:T(8,128)(2,1)S(1)}, u32[]{:S(2)}, u32[]{:S(2)}) collective-permute-start(bf16[4,2,80,128]{3,2,1,0:T(8,128)(2,1)S(1)} %pad_maximum_fusion.2), channel_id=1, source_target_pairs={{0,2},{1,3},{2,0},{3,1},{4,6},{5,7},{6,4},{7,5},{8,10},{9,11},{10,... | collective-permute-start | bytes 491528 | tf_op jit(solution)/shard_map/ppermute | solution.py:492
  58.9 0.1 collective-permute-start.3
  58.9 0.1 broadcast_in_dim.7
  59.0 0.1 broadcast_in_dim.8.azim_ref
  59.2 4.7 %tables.1 = (bf16[256,1408]{1,0:T(8,128)(2,1)S(1)}, bf16[256,1280]{1,0:T(8,128)(2,1)S(1)}, bf16[384,1408]{1,0:T(8,128)(2,1)S(1)}, bf16[384,1280]{1,0:T(8,128)(2,1)S(1)}) custom-call(s32[16,40,128]{2,1,0:T(8,128)S(1)} %broadcast_in_dim.8.azim_ref), custom_call_target="tpu_custom_call" | custom-call | tf_op jit(solution)/shard_map/tables/pallas_call | solution.py:360
  63.9 1.0 %copy-done = bf16[384,1408]{1,0:T(8,128)(2,1)} copy-done((bf16[384,1408]{1,0:T(8,128)(2,1)}, bf16[384,1408]{1,0:T(8,128)(2,1)S(1)}, u32[]{:S(2)}) %copy-start) | copy-done | bytes 1081368
  64.9 1.0 %copy-done.1 = bf16[384,1280]{1,0:T(8,128)(2,1)} copy-done((bf16[384,1280]{1,0:T(8,128)(2,1)}, bf16[384,1280]{1,0:T(8,128)(2,1)S(1)}, u32[]{:S(2)}) %copy-start.1) | copy-done | bytes 983064
  65.8 0.9 %copy-done.2 = bf16[256,1408]{1,0:T(8,128)(2,1)} copy-done((bf16[256,1408]{1,0:T(8,128)(2,1)}, bf16[256,1408]{1,0:T(8,128)(2,1)S(1)}, u32[]{:S(2)}) %copy-start.2) | copy-done | bytes 720920
  66.7 0.8 %copy-done.3 = bf16[256,1280]{1,0:T(8,128)(2,1)} copy-done((bf16[256,1280]{1,0:T(8,128)(2,1)}, bf16[256,1280]{1,0:T(8,128)(2,1)S(1)}, u32[]{:S(2)}) %copy-start.3) | copy-done | bytes 655384
  67.6 0.0 collective-permute-done.5
  67.6 0.0 collective-permute-done.4
  67.6 0.0 all-to-all-done
  67.6 6.7 %grid_product.1 = bf16[8,10,8,2560]{3,2,1,0:T(8,128)(2,1)} custom-call(bf16[4,2,5,16,128]{4,3,2,1,0:T(8,128)(2,1)S(1)} %bitcast.8, bf16[4,2,5,16,128]{4,3,2,1,0:T(8,128)(2,1)S(1)} %bitcast.11, bf16[4,2,5,16,128]{4,3,2,1,0:T(8,128)(2,1)S(1)} %bitcast.10, bf16[4,2,5,16,128]{4,3,2,1,0:T(8,128)(2,1)S(1)} %bitcast.9, bf16[16,3,5,16,128]{4,3,2,1,0:T(8,128)(2,1)S(1)} %bitcast.7, ...), custom_call_target="tpu_custom_call" | custom-call | tf_op jit(solution)/shard_map/grid_product/pallas_call | solution.py:463
  (14 shorter events, 0.2 us)
Async XLA Ops:
  12.6 46.4 %copy-start.4 = (s32[640]{0:T(1024)S(1)}, s32[640]{0:T(1024)}, u32[]{:S(2)}) copy-start(s32[640]{0:T(1024)} %refs_0_.3) | copy-start | bytes 7684
  12.6 55.0 %all-to-all-start = ((bf16[16,3,80,128]{3,2,1,0:T(8,128)(2,1)}), bf16[16,3,80,128]{3,2,1,0:T(8,128)(2,1)S(1)}, u32[]{:S(2)}, u32[]{:S(2)}) async-start(bf16[16,3,80,128]{3,2,1,0:T(8,128)(2,1)} %legendre.3), calls=%async_computation | async-start | bytes 1966080 | tf_op jit(solution)/shard_map/all_to_all | solution.py:501
  19.1 20.6 %collective-permute-start = (bf16[4,2,80,128]{3,2,1,0:T(8,128)(2,1)S(1)}, bf16[4,2,80,128]{3,2,1,0:T(8,128)(2,1)S(1)}, u32[]{:S(2)}, u32[]{:S(2)}) collective-permute-start(bf16[4,2,80,128]{3,2,1,0:T(8,128)(2,1)S(1)} %get-tuple-element.16), channel_id=1, source_target_pairs={{0,4},{1,5},{2,6},{3,7},{4,0},{5,1},{6,2},{7,3},{8,12},{9,13},{10,... | collective-permute-start | bytes 491528 | tf_op jit(solution)/shard_map/ppermute | solution.py:492
  19.4 31.5 %collective-permute-start.1 = (bf16[4,2,80,128]{3,2,1,0:T(8,128)(2,1)S(1)}, bf16[4,2,80,128]{3,2,1,0:T(8,128)(2,1)S(1)}, u32[]{:S(2)}, u32[]{:S(2)}) collective-permute-start(bf16[4,2,80,128]{3,2,1,0:T(8,128)(2,1)S(1)} %get-tuple-element.17), channel_id=1, source_target_pairs={{0,8},{1,9},{2,10},{3,11},{4,12},{5,13},{6,14},{7,15},{8,0},{9,1},... | collective-permute-start | bytes 491528 | tf_op jit(solution)/shard_map/ppermute | solution.py:492
  21.5 34.8 %collective-permute-start.2 = (bf16[4,2,80,128]{3,2,1,0:T(8,128)(2,1)S(1)}, bf16[4,2,80,128]{3,2,1,0:T(8,128)(2,1)S(1)}, u32[]{:S(2)}, u32[]{:S(2)}) collective-permute-start(bf16[4,2,80,128]{3,2,1,0:T(8,128)(2,1)S(1)} %get-tuple-element.18), channel_id=1, source_target_pairs={{0,12},{1,13},{2,14},{3,15},{4,8},{5,9},{6,10},{7,11},{8,4},{9,5},... | collective-permute-start | bytes 491528 | tf_op jit(solution)/shard_map/ppermute | solution.py:492
  56.4 11.2 %collective-permute-start.5 = (bf16[4,2,80,128]{3,2,1,0:T(8,128)(2,1)S(1)}, bf16[4,2,80,128]{3,2,1,0:T(8,128)(2,1)S(1)}, u32[]{:S(2)}, u32[]{:S(2)}) collective-permute-start(bf16[4,2,80,128]{3,2,1,0:T(8,128)(2,1)S(1)} %pad_maximum_fusion.3), channel_id=1, source_target_pairs={{0,3},{1,2},{2,1},{3,0},{4,7},{5,6},{6,5},{7,4},{8,11},{9,10},{10,... | collective-permute-start | bytes 491528 | tf_op jit(solution)/shard_map/ppermute | solution.py:492
  57.6 10.0 %collective-permute-start.4 = (bf16[4,2,80,128]{3,2,1,0:T(8,128)(2,1)S(1)}, bf16[4,2,80,128]{3,2,1,0:T(8,128)(2,1)S(1)}, u32[]{:S(2)}, u32[]{:S(2)}) collective-permute-start(bf16[4,2,80,128]{3,2,1,0:T(8,128)(2,1)S(1)} %pad_maximum_fusion.2), channel_id=1, source_target_pairs={{0,2},{1,3},{2,0},{3,1},{4,6},{5,7},{6,4},{7,5},{8,10},{9,11},{10,... | collective-permute-start | bytes 491528 | tf_op jit(solution)/shard_map/ppermute | solution.py:492
  58.9 8.7 %collective-permute-start.3 = (bf16[4,2,80,128]{3,2,1,0:T(8,128)(2,1)S(1)}, bf16[4,2,80,128]{3,2,1,0:T(8,128)(2,1)S(1)}, u32[]{:S(2)}, u32[]{:S(2)}) collective-permute-start(bf16[4,2,80,128]{3,2,1,0:T(8,128)(2,1)S(1)} %pad_maximum_fusion.1), channel_id=1, source_target_pairs={{0,1},{1,0},{2,3},{3,2},{4,5},{5,4},{6,7},{7,6},{8,9},{9,8},{10,11... | collective-permute-start | bytes 491528 | tf_op jit(solution)/shard_map/ppermute | solution.py:492
  63.9 1.0 %copy-start = (bf16[384,1408]{1,0:T(8,128)(2,1)}, bf16[384,1408]{1,0:T(8,128)(2,1)S(1)}, u32[]{:S(2)}) copy-start(bf16[384,1408]{1,0:T(8,128)(2,1)S(1)} %get-tuple-element.23.refs_7_) | copy-start | bytes 3244036
  64.9 1.0 %copy-start.1 = (bf16[384,1280]{1,0:T(8,128)(2,1)}, bf16[384,1280]{1,0:T(8,128)(2,1)S(1)}, u32[]{:S(2)}) copy-start(bf16[384,1280]{1,0:T(8,128)(2,1)S(1)} %get-tuple-element.24.refs_8_) | copy-start | bytes 2949124
  65.8 0.9 %copy-start.2 = (bf16[256,1408]{1,0:T(8,128)(2,1)}, bf16[256,1408]{1,0:T(8,128)(2,1)S(1)}, u32[]{:S(2)}) copy-start(bf16[256,1408]{1,0:T(8,128)(2,1)S(1)} %get-tuple-element.21.refs_5_) | copy-start | bytes 2162692
  66.7 0.8 %copy-start.3 = (bf16[256,1280]{1,0:T(8,128)(2,1)}, bf16[256,1280]{1,0:T(8,128)(2,1)S(1)}, u32[]{:S(2)}) copy-start(bf16[256,1280]{1,0:T(8,128)(2,1)S(1)} %get-tuple-element.22.refs_6_) | copy-start | bytes 1966084

commit v7 on v6

--- a/solution.py
+++ b/solution.py
@@ -89,10 +89,15 @@
 
     def load(step, targets):
         at = pl.ds((begin + step) * SUBLANES, SUBLANES)
+        solved = pl.ds(0, 4 * levels)
+        others = pl.ds(4 * levels, rhs_hbm.shape[0] - 4 * levels)
         copies = [
-            pltpu.make_async_copy(rhs_hbm.at[:, at, :], targets[0], load_sem.at[step, 0]),
-            pltpu.make_async_copy(polar_hbm.at[at], targets[1], load_sem.at[step, 1]),
+            pltpu.make_async_copy(
+                rhs_hbm.at[rows, at, :], targets[0].at[rows], load_sem.at[step, i]
+            )
+            for i, rows in enumerate((solved, others))
         ]
+        copies.append(pltpu.make_async_copy(polar_hbm.at[at], targets[1], load_sem.at[step, 2]))
         for copy in copies:
             copy.start()
         return copies
@@ -106,20 +111,28 @@
     for step in range(carried, min(carried + 2, steps)):
         loads[step] = load(step, blocks[step])
 
+    def await_loads(step, begin, end):
+        for copy in loads.get(step, ())[begin:end]:
+            copy.wait()
+
     def arrive(step):
-        for copy in loads.get(step, ()):
-            copy.wait()
+        await_loads(step, 0, 3 if carried else 1)
         after = step + 2
         if after in blocks and after not in loads:
             loads[after] = load(after, blocks[after])
 
     def prepare(step):
         pad = (pad_one, pad_two)[step % 2]
-        yield from update_parts(azim_ref, matrices, blocks[step][0], pad, begin + step, levels)
+        late = None if carried else functools.partial(await_loads, step, 1, 2)
+        yield from update_parts(
+            azim_ref, matrices, blocks[step][0], pad, begin + step, levels, late
+        )
 
     def finish(step):
         pad, nat = ((pad_one, nat_one), (pad_two, nat_two))[step % 2]
         outputs = [stage_ref.at[step, g] for g in range(outs)]
+        if not carried:
+            await_loads(step, 2, 3)
         yield from product_parts(
             azim_ref, arr_ref, blocks[step][1], pad, nat, outputs, begin + step, near
         )
@@ -131,9 +144,9 @@
             )
             stores[-1].start()
 
-    arrive(0)
     for copy in small:
         copy.wait()
+    arrive(0)
     for _ in prepare(0):
         pass
     for step in range(steps):
@@ -141,16 +154,14 @@
         if step + 1 < steps and carried:
             arrive(step + 1)
             following = prepare(step + 1)
-        for _ in finish(step):
+        for part in finish(step):
+            if part == SUBLANES - 1 and step + 1 < steps and not carried:
+                arrive(step + 1)
+                following = prepare(step + 1)
             next(following, None)
         for _ in following:
             pass
-        if step + 1 < steps and not carried:
-            arrive(step + 1)
-            for _ in prepare(step + 1):
-                pass
-    for copy in loads.get(steps, ()):
-        copy.wait()
+    await_loads(steps, 0, 3)
     for copy in stores:
         copy.wait()
 
@@ -160,7 +171,7 @@
     return lax.axis_index("lat") * own + step * SUBLANES
 
 
-def update_parts(azim_ref, matrices, rhs_ref, pad_ref, step, levels):
+def update_parts(azim_ref, matrices, rhs_ref, pad_ref, step, levels, late):
     fwd_ref, back_ref, cel_ref, therm_ref = matrices
     rows, _, waves = rhs_ref.shape
     tiles = waves // LANES
@@ -169,6 +180,11 @@
 
     def rhs(row, t):
         return rhs_ref[row, :, t * LANES : (t + 1) * LANES]
+
+    def move(ts):
+        for t in ts:
+            for row in range(4 * levels, rows):
+                pad_ref[t, pl.ds(row * pitch, SUBLANES), :] = rhs(row, t)
 
     sub = lax.broadcasted_iota(jnp.int32, (SUBLANES, LANES), 0)
     lane = lax.broadcasted_iota(jnp.int32, (SUBLANES, LANES), 1)
@@ -207,9 +223,12 @@
             for i, (t, c) in enumerate(parts):
                 row = (levels + l) * 2 + c
                 pad_ref[t, pl.ds(row * pitch, SUBLANES), :] = rhs(row, t) - response[i]
-        for t in ts:
-            for row in range(4 * levels, rows):
-                pad_ref[t, pl.ds(row * pitch, SUBLANES), :] = rhs(row, t)
+        if late is None:
+            move(ts)
+        yield
+    if late is not None:
+        late()
+        move(range(tiles))
         yield
 
 
@@ -236,12 +255,14 @@
             polar_ref[s], coeffs, (((1,), (1,)), ((), ())), preferred_element_type=jnp.float32
         )
         nat_ref[pl.ds(s * apart, nlat), :] = product
-        yield
+        yield s
 
     half = LANES // 2
     low = lax.broadcasted_iota(jnp.int32, (SUBLANES, LANES), 1) < half
     pairs = out_refs[0].shape[1] // (2 * SUBLANES)
     for p in range(nlat // 2):
+        if near and p % (nlat // 8) == 0 and p:
+            yield
         d, q = divmod(p, pairs)
         at = ((mine ^ d if near else d) * pairs + q) * 2
         a = nat_ref[pl.ds(arr_ref[at], SUBLANES, stride=apart), :]
@@ -304,7 +325,7 @@
         + [
             pltpu.VMEM((steps, outs, group, depth, LANES), jnp.bfloat16),
             pltpu.SemaphoreType.DMA((len(scalars),)),
-            pltpu.SemaphoreType.DMA((steps + 1, 2)),
+            pltpu.SemaphoreType.DMA((steps + 1, 3)),
             pltpu.SemaphoreType.DMA((steps, outs)),
         ],
         compiler_params=pltpu.CompilerParams(vmem_limit_bytes=VMEM_MIB * 1024 * 1024),
@@ -370,11 +391,43 @@
     )(spread)
 
 
+def turn(x, real_ref, imag_ref, p, at):
+    rows = x.astype(jnp.float32)
+    count = rows.shape[0] * rows.shape[1] * SUBLANES
+    for c, ref in enumerate((real_ref, imag_ref)):
+        part = rows[:, :, c * SUBLANES : (c + 1) * SUBLANES].reshape(count, LANES)
+        ref[pl.ds(p * LANES, LANES), pl.ds(at, count)] = part.astype(jnp.bfloat16).T
+
+
+def turn_kernel(*refs):
+    *parts, real_ref, imag_ref = refs
+    for p in range(parts[0].shape[2]):
+        turn(jnp.concatenate([ref[:, :, p] for ref in parts], 0), real_ref, imag_ref, p, 0)
+
+
+def split_pairs(x, lat_dev):
+    return x.reshape(*x.shape[:2], lat_dev // 2, 2 * SUBLANES, LANES)
+
+
+def turned(early, lat_dev):
+    parts = [split_pairs(x, lat_dev) for x in early]
+    depth = sum(x.shape[0] * x.shape[1] * SUBLANES for x in early)
+    vmem = pl.BlockSpec(memory_space=pltpu.VMEM)
+    return pl.pallas_call(
+        turn_kernel,
+        in_specs=[vmem] * len(parts),
+        out_specs=[vmem] * 2,
+        out_shape=[jax.ShapeDtypeStruct((lat_dev * LANES // 2, depth), jnp.bfloat16)] * 2,
+        compiler_params=pltpu.CompilerParams(vmem_limit_bytes=16 * 1024 * 1024),
+        name="turn",
+    )(*parts)
+
+
 def grid_kernel(
-    *refs, near, fields, lat_dev, block
+    *refs, fields, lat_dev, block
 ):
-    early_refs, late_ref, tables, out_hbm = refs[:near], refs[near], refs[near + 1 : near + 5], refs[near + 5]
-    cos_ref, sin_ref, real_ref, imag_ref, out_ref, load_sem, out_sem = refs[near + 6 :]
+    early_refs, late_ref, tables, out_hbm = refs[:2], refs[2], refs[3:7], refs[7]
+    cos_ref, sin_ref, real_ref, imag_ref, out_ref, load_sem, out_sem = refs[8:]
     width = sin_ref.shape[1]
     early = tables[0].shape[0]
     nlon = 2 * width
@@ -402,16 +455,10 @@
     ends = load(len(order), tail, (0, 2))
     loads = {i: load(i, span(i), range(4)) for i in order}
 
+    real_ref[:, :early] = early_refs[0][...]
+    imag_ref[:, :early] = early_refs[1][...]
     for p in range(lat_dev // 2):
-        first = jnp.concatenate([ref[:, :, p] for ref in early_refs], 0).astype(jnp.float32)
-        later = late_ref[:, :, p].astype(jnp.float32)
-        at = 0
-        for rows in (first, later):
-            count = rows.shape[0] * rows.shape[1] * SUBLANES
-            for c, ref in enumerate((real_ref, imag_ref)):
-                part = rows[:, :, c * SUBLANES : (c + 1) * SUBLANES].reshape(count, LANES)
-                ref[pl.ds(p * LANES, LANES), pl.ds(at, count)] = part.astype(jnp.bfloat16).T
-            at += count
+        turn(late_ref[:, :, p], real_ref, imag_ref, p, early)
 
     lane = lax.broadcasted_iota(jnp.int32, (lat_dev * half, LANES), 1)
     mirror = (LANES - lane) % LANES
@@ -428,12 +475,12 @@
         far = even - odd
         tiles = block // LANES
         parts = [far[:, t * LANES : (t + 1) * LANES] for t in range(tiles)] + [after]
-        turned = [
+        flipped = [
             jnp.where(lane == 0, parts[t + 1], jnp.take_along_axis(parts[t], mirror, axis=1))
             for t in range(tiles)
         ]
         after = parts[0]
-        for q, value in enumerate((near, jnp.concatenate(turned[::-1], 1))):
+        for q, value in enumerate((near, jnp.concatenate(flipped[::-1], 1))):
             for r in range(lat_dev):
                 for f in range(fields):
                     row = r * half + f * levels
@@ -450,18 +497,15 @@
 
 
 def grid_product(early, late, tabs, lat_dev, fields, block=256):
-    near = len(early)
     width = tabs[1].shape[1]
     depth = tabs[1].shape[0] + tabs[3].shape[0]
     half = LANES // 2
     levels = half // fields
     count = width // block
-    parts = [
-        x.reshape(*x.shape[:2], lat_dev // 2, 2 * SUBLANES, LANES) for x in (*early, late)
-    ]
+    parts = [*early, split_pairs(late, lat_dev)]
     hbm = pl.BlockSpec(memory_space=pltpu.HBM)
     out = pl.pallas_call(
-        functools.partial(grid_kernel, near=near, fields=fields, lat_dev=lat_dev, block=block),
+        functools.partial(grid_kernel, fields=fields, lat_dev=lat_dev, block=block),
         in_specs=[pl.BlockSpec(memory_space=pltpu.VMEM)] * len(parts) + [hbm] * len(tabs),
         out_specs=hbm,
         out_shape=jax.ShapeDtypeStruct((fields, lat_dev, levels, 2 * width), jnp.bfloat16),
@@ -503,6 +547,7 @@
     for j in range(NEAR):
         part = jnp.concatenate([x[j : j + 1] for x in got], 0)
         early.append(swap(part, j) if j else part)
+    early = turned(early, lat_dev)
     tabs = tables(azimuthal, devices, EARLY * SUBLANES, NEAR)
     return grid_product(early, late, tabs, lat_dev, fields)
 

time: 74.9 us -> 74.3 us (level)
    pallas_call x1 -> x2, Pallas kernels: 6.72 us -> 6.61 us  [the longest x1 6.39 us: grid_product(): pl.pallas_call(functools.partial(grid_kernel, fields=fields, lat_dev=lat_...]
  transfers between devices with their start and end apart: 7 -> 7, of which waited for: 3 -> 3; matrix products, arithmetic and copies ran while one was open for 0% -> 0% of each run, Pallas kernels for 6% -> 7%
where the time goes in v7:
time: 74.3 us; the launch traced here: 73.9 us
  waiting for transfers between devices  34.5 us (46%)
  Pallas kernels  23.3 us (31%)
  starting transfers between devices  11.8 us (16%)
  local copies, waits for them, and re-layouts  3.93 us (5%)
    ppermute x6, waiting for transfers between devices, swap(): return lax.ppermute(x, 'lat', [(d, d ^ distance) for d in range(devices)])  34.5 us
    pallas_call x2, Pallas kernels, legendre(): pl.pallas_call(functools.partial(legendre_kernel, levels=levels, begin=be...  12 us
    all_to_all x1, starting transfers between devices, per_device(): lax.all_to_all(packed, 'lat', split_axis=0, concat_axis=0, tiled=True)  6.53 us
    pallas_call x1, Pallas kernels, grid_product(): pl.pallas_call(functools.partial(grid_kernel, fields=fields, lat_dev=lat_...  6.39 us
    ppermute x6, starting transfers between devices, swap(): return lax.ppermute(x, 'lat', [(d, d ^ distance) for d in range(devices)])  5.23 us
    pallas_call x1, Pallas kernels, tables(): pl.pallas_call(functools.partial(table_kernel, nlon=NLON, early=early, ne...  4.68 us
    unnamed x10, local copies, waits for them, and re-layouts  3.66 us
  transfers between devices with their start and end apart: 7, of which 3 were waited for; matrix products, arithmetic and copies ran while one was open for 0% of the time, Pallas kernels for 7%

profile of v7, /device:TPU:13, one launch (start us, length us, event | category | flops | bytes accessed | tf_op | source)
XLA Modules:
  0.0 73.9 jit_solution(5598174721007522288)
XLA Ops:
  0.0 5.3 %legendre.2 = (bf16[4,2,80,128]{3,2,1,0:T(8,128)(2,1)S(1)}, bf16[4,2,80,128]{3,2,1,0:T(8,128)(2,1)S(1)}, bf16[4,2,80,128]{3,2,1,0:T(8,128)(2,1)S(1)}, bf16[4,2,8...) custom-call(s32[640]{0:T(1024)} %refs_0_.3, s32[160]{0:T(256)} %refs_1_.3, ...), custom_call_target="tpu_custom_call" | custom-call | tf_op jit(solution)/shard_map/legendre/pallas_call | solution.py:309
  5.3 6.7 %legendre.3 = bf16[16,3,80,128]{3,2,1,0:T(8,128)(2,1)} custom-call(s32[640]{0:T(1024)} %refs_0_.3, s32[160]{0:T(256)} %refs_1_.3, f32[8,8]{1,0:T(8,128)} %refs_2_.3, f32[8,8]{1,0:T(8,128)} %refs_3_.3, f32[8]{0:T(128)} %refs_4_.3, f32[8,8]{1,0:T(8,128)} %refs_5_.3, f32[128,40,640]{2,1,0:T(8,128)} %bitcast.13, bf16[40,160,640]{2,1,0:T(8,128)(2,1)} %refs_7_.3, ...), custom_call_target="tpu_custom_call" | custom-call | tf_op jit(solution)/shard_map/legendre/pallas_call | solution.py:309
  12.0 0.0 copy-start.4
  12.1 6.5 %all-to-all-start = ((bf16[16,3,80,128]{3,2,1,0:T(8,128)(2,1)}), bf16[16,3,80,128]{3,2,1,0:T(8,128)(2,1)S(1)}, u32[]{:S(2)}, u32[]{:S(2)}) async-start(bf16[16,3,80,128]{3,2,1,0:T(8,128)(2,1)} %legendre.3), calls=%async_computation | async-start | bytes 1966080 | tf_op jit(solution)/shard_map/all_to_all | solution.py:545
  18.6 0.3 collective-permute-start
  18.9 2.1 %collective-permute-start.1 = (bf16[4,2,80,128]{3,2,1,0:T(8,128)(2,1)S(1)}, bf16[4,2,80,128]{3,2,1,0:T(8,128)(2,1)S(1)}, u32[]{:S(2)}, u32[]{:S(2)}) collective-permute-start(bf16[4,2,80,128]{3,2,1,0:T(8,128)(2,1)S(1)} %get-tuple-element.19), channel_id=1, source_target_pairs={{0,8},{1,9},{2,10},{3,11},{4,12},{5,13},{6,14},{7,15},{8,0},{9,1},... | collective-permute-start | bytes 491528 | tf_op jit(solution)/shard_map/ppermute | solution.py:536
  21.0 0.3 collective-permute-start.2
  21.3 17.8 %collective-permute-done = bf16[4,2,80,128]{3,2,1,0:T(8,128)(2,1)S(1)} collective-permute-done((bf16[4,2,80,128]{3,2,1,0:T(8,128)(2,1)S(1)}, bf16[4,2,80,128]{3,2,1,0:T(8,128)(2,1)S(1)}, u32[]{:S(2)}, u32[]{:S(2)}) %collective-permute-start) | collective-permute-done | bytes 163872 | tf_op jit(solution)/shard_map/ppermute | solution.py:536
  39.2 11.3 %collective-permute-done.1 = bf16[4,2,80,128]{3,2,1,0:T(8,128)(2,1)S(1)} collective-permute-done((bf16[4,2,80,128]{3,2,1,0:T(8,128)(2,1)S(1)}, bf16[4,2,80,128]{3,2,1,0:T(8,128)(2,1)S(1)}, u32[]{:S(2)}, u32[]{:S(2)}) %collective-permute-start.1) | collective-permute-done | bytes 163872 | tf_op jit(solution)/shard_map/ppermute | solution.py:536
  50.4 5.4 %collective-permute-done.2 = bf16[4,2,80,128]{3,2,1,0:T(8,128)(2,1)S(1)} collective-permute-done((bf16[4,2,80,128]{3,2,1,0:T(8,128)(2,1)S(1)}, bf16[4,2,80,128]{3,2,1,0:T(8,128)(2,1)S(1)}, u32[]{:S(2)}, u32[]{:S(2)}) %collective-permute-start.2) | collective-permute-done | bytes 163872 | tf_op jit(solution)/shard_map/ppermute | solution.py:536
  55.9 1.2 %collective-permute-start.5 = (bf16[4,2,80,128]{3,2,1,0:T(8,128)(2,1)S(1)}, bf16[4,2,80,128]{3,2,1,0:T(8,128)(2,1)S(1)}, u32[]{:S(2)}, u32[]{:S(2)}) collective-permute-start(bf16[4,2,80,128]{3,2,1,0:T(8,128)(2,1)S(1)} %pad_maximum_fusion.3), channel_id=1, source_target_pairs={{0,3},{1,2},{2,1},{3,0},{4,7},{5,6},{6,5},{7,4},{8,11},{9,10},{10,... | collective-permute-start | bytes 491528 | tf_op jit(solution)/shard_map/ppermute | solution.py:536
  57.1 1.2 %collective-permute-start.4 = (bf16[4,2,80,128]{3,2,1,0:T(8,128)(2,1)S(1)}, bf16[4,2,80,128]{3,2,1,0:T(8,128)(2,1)S(1)}, u32[]{:S(2)}, u32[]{:S(2)}) collective-permute-start(bf16[4,2,80,128]{3,2,1,0:T(8,128)(2,1)S(1)} %pad_maximum_fusion.2), channel_id=1, source_target_pairs={{0,2},{1,3},{2,0},{3,1},{4,6},{5,7},{6,4},{7,5},{8,10},{9,11},{10,... | collective-permute-start | bytes 491528 | tf_op jit(solution)/shard_map/ppermute | solution.py:536
  58.4 0.1 collective-permute-start.3
  58.4 0.1 broadcast_in_dim.7
  58.5 0.1 broadcast_in_dim.8.azim_ref
  58.7 4.7 %tables.1 = (bf16[256,1408]{1,0:T(8,128)(2,1)S(1)}, bf16[256,1280]{1,0:T(8,128)(2,1)S(1)}, bf16[384,1408]{1,0:T(8,128)(2,1)S(1)}, bf16[384,1280]{1,0:T(8,128)(2,1)S(1)}) custom-call(s32[16,40,128]{2,1,0:T(8,128)S(1)} %broadcast_in_dim.8.azim_ref), custom_call_target="tpu_custom_call" | custom-call | tf_op jit(solution)/shard_map/tables/pallas_call | solution.py:381
  63.4 1.0 %copy-done = bf16[384,1408]{1,0:T(8,128)(2,1)} copy-done((bf16[384,1408]{1,0:T(8,128)(2,1)}, bf16[384,1408]{1,0:T(8,128)(2,1)S(1)}, u32[]{:S(2)}) %copy-start) | copy-done | bytes 1081368
  64.4 1.0 %copy-done.1 = bf16[384,1280]{1,0:T(8,128)(2,1)} copy-done((bf16[384,1280]{1,0:T(8,128)(2,1)}, bf16[384,1280]{1,0:T(8,128)(2,1)S(1)}, u32[]{:S(2)}) %copy-start.1) | copy-done | bytes 983064
  65.3 0.9 %copy-done.2 = bf16[256,1408]{1,0:T(8,128)(2,1)} copy-done((bf16[256,1408]{1,0:T(8,128)(2,1)}, bf16[256,1408]{1,0:T(8,128)(2,1)S(1)}, u32[]{:S(2)}) %copy-start.2) | copy-done | bytes 720920
  66.2 0.8 %copy-done.3 = bf16[256,1280]{1,0:T(8,128)(2,1)} copy-done((bf16[256,1280]{1,0:T(8,128)(2,1)}, bf16[256,1280]{1,0:T(8,128)(2,1)S(1)}, u32[]{:S(2)}) %copy-start.3) | copy-done | bytes 655384
  67.1 0.0 collective-permute-done.3
  67.1 0.2 turn.1
  67.3 0.0 all-to-all-done
  67.3 6.4 %grid_product.1 = bf16[8,10,8,2560]{3,2,1,0:T(8,128)(2,1)} custom-call(bf16[640,256]{1,0:T(8,128)(2,1)S(1)} %get-tuple-element.21.refs_0_, bf16[640,256]{1,0:T(8,128)(2,1)S(1)} %get-tuple-element.22.refs_1_, bf16[16,3,5,16,128]{4,3,2,1,0:T(8,128)(2,1)S(1)} %bitcast.7, bf16[256,1408]{1,0:T(8,128)(2,1)} %copy-done.2, bf16[256,1280]{1,0:T(8,128)(2,1)} %copy-done.3, ...), custom_call_target="tpu_custom_call" | custom-call | tf_op jit(solution)/shard_map/grid_product/pallas_call | solution.py:507
  (15 shorter events, 0.2 us)
Async XLA Ops:
  12.0 46.4 %copy-start.4 = (s32[640]{0:T(1024)S(1)}, s32[640]{0:T(1024)}, u32[]{:S(2)}) copy-start(s32[640]{0:T(1024)} %refs_0_.3) | copy-start | bytes 7684
  12.1 55.3 %all-to-all-start = ((bf16[16,3,80,128]{3,2,1,0:T(8,128)(2,1)}), bf16[16,3,80,128]{3,2,1,0:T(8,128)(2,1)S(1)}, u32[]{:S(2)}, u32[]{:S(2)}) async-start(bf16[16,3,80,128]{3,2,1,0:T(8,128)(2,1)} %legendre.3), calls=%async_computation | async-start | bytes 1966080 | tf_op jit(solution)/shard_map/all_to_all | solution.py:545
  18.6 20.6 %collective-permute-start = (bf16[4,2,80,128]{3,2,1,0:T(8,128)(2,1)S(1)}, bf16[4,2,80,128]{3,2,1,0:T(8,128)(2,1)S(1)}, u32[]{:S(2)}, u32[]{:S(2)}) collective-permute-start(bf16[4,2,80,128]{3,2,1,0:T(8,128)(2,1)S(1)} %get-tuple-element.18), channel_id=1, source_target_pairs={{0,4},{1,5},{2,6},{3,7},{4,0},{5,1},{6,2},{7,3},{8,12},{9,13},{10,... | collective-permute-start | bytes 491528 | tf_op jit(solution)/shard_map/ppermute | solution.py:536
  18.9 31.5 %collective-permute-start.1 = (bf16[4,2,80,128]{3,2,1,0:T(8,128)(2,1)S(1)}, bf16[4,2,80,128]{3,2,1,0:T(8,128)(2,1)S(1)}, u32[]{:S(2)}, u32[]{:S(2)}) collective-permute-start(bf16[4,2,80,128]{3,2,1,0:T(8,128)(2,1)S(1)} %get-tuple-element.19), channel_id=1, source_target_pairs={{0,8},{1,9},{2,10},{3,11},{4,12},{5,13},{6,14},{7,15},{8,0},{9,1},... | collective-permute-start | bytes 491528 | tf_op jit(solution)/shard_map/ppermute | solution.py:536
  21.0 34.8 %collective-permute-start.2 = (bf16[4,2,80,128]{3,2,1,0:T(8,128)(2,1)S(1)}, bf16[4,2,80,128]{3,2,1,0:T(8,128)(2,1)S(1)}, u32[]{:S(2)}, u32[]{:S(2)}) collective-permute-start(bf16[4,2,80,128]{3,2,1,0:T(8,128)(2,1)S(1)} %get-tuple-element.20), channel_id=1, source_target_pairs={{0,12},{1,13},{2,14},{3,15},{4,8},{5,9},{6,10},{7,11},{8,4},{9,5},... | collective-permute-start | bytes 491528 | tf_op jit(solution)/shard_map/ppermute | solution.py:536
  55.9 11.2 %collective-permute-start.5 = (bf16[4,2,80,128]{3,2,1,0:T(8,128)(2,1)S(1)}, bf16[4,2,80,128]{3,2,1,0:T(8,128)(2,1)S(1)}, u32[]{:S(2)}, u32[]{:S(2)}) collective-permute-start(bf16[4,2,80,128]{3,2,1,0:T(8,128)(2,1)S(1)} %pad_maximum_fusion.3), channel_id=1, source_target_pairs={{0,3},{1,2},{2,1},{3,0},{4,7},{5,6},{6,5},{7,4},{8,11},{9,10},{10,... | collective-permute-start | bytes 491528 | tf_op jit(solution)/shard_map/ppermute | solution.py:536
  57.1 10.0 %collective-permute-start.4 = (bf16[4,2,80,128]{3,2,1,0:T(8,128)(2,1)S(1)}, bf16[4,2,80,128]{3,2,1,0:T(8,128)(2,1)S(1)}, u32[]{:S(2)}, u32[]{:S(2)}) collective-permute-start(bf16[4,2,80,128]{3,2,1,0:T(8,128)(2,1)S(1)} %pad_maximum_fusion.2), channel_id=1, source_target_pairs={{0,2},{1,3},{2,0},{3,1},{4,6},{5,7},{6,4},{7,5},{8,10},{9,11},{10,... | collective-permute-start | bytes 491528 | tf_op jit(solution)/shard_map/ppermute | solution.py:536
  58.4 8.7 %collective-permute-start.3 = (bf16[4,2,80,128]{3,2,1,0:T(8,128)(2,1)S(1)}, bf16[4,2,80,128]{3,2,1,0:T(8,128)(2,1)S(1)}, u32[]{:S(2)}, u32[]{:S(2)}) collective-permute-start(bf16[4,2,80,128]{3,2,1,0:T(8,128)(2,1)S(1)} %pad_maximum_fusion.1), channel_id=1, source_target_pairs={{0,1},{1,0},{2,3},{3,2},{4,5},{5,4},{6,7},{7,6},{8,9},{9,8},{10,11... | collective-permute-start | bytes 491528 | tf_op jit(solution)/shard_map/ppermute | solution.py:536
  63.4 1.0 %copy-start = (bf16[384,1408]{1,0:T(8,128)(2,1)}, bf16[384,1408]{1,0:T(8,128)(2,1)S(1)}, u32[]{:S(2)}) copy-start(bf16[384,1408]{1,0:T(8,128)(2,1)S(1)} %get-tuple-element.27.refs_5_) | copy-start | bytes 3244036
  64.4 1.0 %copy-start.1 = (bf16[384,1280]{1,0:T(8,128)(2,1)}, bf16[384,1280]{1,0:T(8,128)(2,1)S(1)}, u32[]{:S(2)}) copy-start(bf16[384,1280]{1,0:T(8,128)(2,1)S(1)} %get-tuple-element.28.refs_6_) | copy-start | bytes 2949124
  65.3 0.9 %copy-start.2 = (bf16[256,1408]{1,0:T(8,128)(2,1)}, bf16[256,1408]{1,0:T(8,128)(2,1)S(1)}, u32[]{:S(2)}) copy-start(bf16[256,1408]{1,0:T(8,128)(2,1)S(1)} %get-tuple-element.25.refs_3_) | copy-start | bytes 2162692
  66.2 0.8 %copy-start.3 = (bf16[256,1280]{1,0:T(8,128)(2,1)}, bf16[256,1280]{1,0:T(8,128)(2,1)S(1)}, u32[]{:S(2)}) copy-start(bf16[256,1280]{1,0:T(8,128)(2,1)S(1)} %get-tuple-element.26.refs_4_) | copy-start | bytes 1966084
